TPU v7x, 32 devices: a whole 2x2x4 slice. The times are simulated.
32 devices in a mesh: row: 4 (over y, x), col: 8 (over z, core).
Axes of the slice: x: 2, y: 2, z: 4, core: 2. Of those that a mesh axis runs over, the one named last changes fastest.
Arguments:
- left_points: float32 [2048, 128], P(('row', 'col')), may hold values from -3.3 to 3.3
- right_points: float32 [2048, 128], P(('row', 'col')), may hold values from -3.3 to 3.3
- left_cotangent: bfloat16 [2048, 128], P(('row', 'col')), may hold values from -6 to 6
- right_coefficient: bfloat16 [2048, 128], P(('row', 'col')), may hold values from -6 to 6
Outputs:
- left_final: float32 [2048, 128], P(('row', 'col'))
- right_final: float32 [2048, 128], P(('row', 'col'))
- left_grad: float32 [2048, 128], P(('row', 'col'))
- right_grad: float32 [2048, 128], P(('row', 'col'))
All inputs are finite; a program needn't handle non-finite values.
Results may differ from a plain program's by a relative error of at most 0.019.
Values may be sent and summed in bfloat16 or wider, within the bound.
No kernel may reach another device: no remote copies, remote signals or barrier semaphores. Data moves between devices by JAX's collectives and lax.ppermute only.
A program may use at most 64 MiB of HBM per device.

v0:
```python
import jax
import jax.numpy as jnp
from jax import lax
from jax.sharding import PartitionSpec as P

STEPS = 2


inverse_width = 0.03125
grad_scale = 0.0625
descent_rate = 0.3


def tile_terms(left_bf, left_panel, right_bf, right_panel):
    left_rows = left_bf.shape[0]
    block_rows = min(512, left_rows)
    block_count = left_rows // block_rows
    feature_width = left_bf.shape[1]
    right_wide = right_bf.astype(jnp.float32)
    right_norm = jnp.sum(right_wide * right_wide, axis=1)
    contract_last = (((1,), (1,)), ((), ()))

    def visit_block(carried, pieces):
        accumulated, column_sum = carried
        piece_feat, piece_panel = pieces
        piece_wide = piece_feat.astype(jnp.float32)
        left_norm = jnp.sum(piece_wide * piece_wide, axis=1)
        crossed = lax.dot_general(
            piece_feat, right_bf, contract_last, preferred_element_type=jnp.float32
        )
        distance = left_norm[:, None] + right_norm[None, :] - 2.0 * crossed
        kernel = jnp.exp(-inverse_width * distance).astype(jnp.bfloat16)
        weight = lax.dot_general(
            piece_panel, right_panel, contract_last, preferred_element_type=jnp.float32
        )
        product = (weight * kernel.astype(jnp.float32)).astype(jnp.bfloat16)
        product_wide = product.astype(jnp.float32)
        left_term = (
            jnp.dot(product, right_bf, preferred_element_type=jnp.float32)
            - jnp.sum(product_wide, axis=1)[:, None] * piece_wide
        )
        accumulated = accumulated + lax.dot_general(
            product, piece_feat, (((0,), (0,)), ((), ())), preferred_element_type=jnp.float32
        )
        column_sum = column_sum + jnp.sum(product_wide, axis=0)
        return ((accumulated, column_sum), left_term)

    initial = (
        jnp.zeros((right_bf.shape[0], feature_width), jnp.float32),
        jnp.zeros((right_bf.shape[0],), jnp.float32),
    )
    pieces = (
        left_bf.reshape(block_count, block_rows, feature_width),
        left_panel.reshape(block_count, block_rows, left_panel.shape[1]),
    )
    (accumulated, column_sum), left_terms = lax.scan(visit_block, initial, pieces)
    return (
        left_terms.reshape(left_rows, feature_width),
        accumulated - column_sum[:, None] * right_wide,
    )


def body(left_points, right_points, left_cotangent, right_coefficient):
    left_panel = lax.all_gather(left_cotangent, "col", axis=0, tiled=True)
    right_panel = lax.all_gather(right_coefficient, "row", axis=0, tiled=True)
    left_own = left_points
    right_own = right_points
    left_grad = jnp.zeros_like(left_points)
    right_grad = jnp.zeros_like(right_points)
    for step_index in range(STEPS):
        left_bf = lax.all_gather(left_own.astype(jnp.bfloat16), "col", axis=0, tiled=True)
        right_bf = lax.all_gather(right_own.astype(jnp.bfloat16), "row", axis=0, tiled=True)
        left_term, right_term = tile_terms(left_bf, left_panel, right_bf, right_panel)
        if step_index + 1 < STEPS:
            left_step = (
                lax.psum_scatter(left_term, "col", scatter_dimension=0, tiled=True) * grad_scale
            )
            right_step = (
                lax.psum_scatter(right_term, "row", scatter_dimension=0, tiled=True) * grad_scale
            )
            left_own = left_own - descent_rate * left_step
            right_own = right_own - descent_rate * right_step
        else:
            left_grad = (
                lax.psum_scatter(left_term, "col", scatter_dimension=0, tiled=True) * grad_scale
            )
            right_grad = (
                lax.psum_scatter(right_term, "row", scatter_dimension=0, tiled=True) * grad_scale
            )
            left_own = left_own - descent_rate * left_grad
            right_own = right_own - descent_rate * right_grad
    return (left_own, right_own, left_grad, right_grad)


def solution(mesh):
    in_specs = (
        P(("row", "col"), None),
        P(("row", "col"), None),
        P(("row", "col"), None),
        P(("row", "col"), None),
    )
    out_specs = (
        P(("row", "col"), None),
        P(("row", "col"), None),
        P(("row", "col"), None),
        P(("row", "col"), None),
    )
    return jax.shard_map(body, mesh=mesh, in_specs=in_specs, out_specs=out_specs, check_vma=False)
```

profile of v0, /device:TPU:0, one launch (start us, length us, event | category | flops | bytes accessed | tf_op | source)
XLA Modules:
  0.0 192.4 jit_solution(17256480161499986418)
XLA Ops:
  7.2 15.9 %all_gather.18 = bf16[512,128]{1,0:T(8,128)(2,1)S(1)} all-gather(bf16[64,128]{1,0:T(8,128)(2,1)} %param.6), channel_id=1, replica_groups=mesh['row'=4,'col'=8] {'col'}, dimensions={0}, use_global_device_ids=true | all-gather | bytes 147456 | tf_op jit(solution)/shard_map/all_gather | solution.py:64
  23.2 8.4 %all_gather.19 = bf16[256,128]{1,0:T(8,128)(2,1)S(1)} all-gather(bf16[64,128]{1,0:T(8,128)(2,1)S(1)} %copy-done.4), channel_id=1, replica_groups=mesh['row'=4,'col'=8] {'row'}, dimensions={0}, use_global_device_ids=true | all-gather | bytes 81920 | tf_op jit(solution)/shard_map/all_gather | solution.py:65
  31.6 14.0 %all_gather.20 = bf16[512,128]{1,0:T(8,128)(2,1)S(1)} all-gather(bf16[64,128]{1,0:T(8,128)(2,1)S(1)} %convert_element_type.58), channel_id=1, replica_groups=mesh['row'=4,'col'=8] {'col'}, dimensions={0}, use_global_device_ids=true | all-gather | bytes 147456 | tf_op jit(solution)/shard_map/all_gather | solution.py:71
  45.6 8.2 %all_gather.21 = bf16[256,128]{1,0:T(8,128)(2,1)S(1)} all-gather(bf16[64,128]{1,0:T(8,128)(2,1)S(1)} %convert_element_type.60), channel_id=1, replica_groups=mesh['row'=4,'col'=8] {'row'}, dimensions={0}, use_global_device_ids=true | all-gather | bytes 81920 | tf_op jit(solution)/shard_map/all_gather | solution.py:72
  53.9 0.1 fusion.14
  54.1 0.2 fusion.20
  54.3 0.4 convert_reduce_fusion.2
  54.7 0.9 convolution_subtract_fusion.3
  55.7 0.9 convolution_subtract_fusion.1
  56.7 23.2 %reduce-scatter.7.cloned.1.call-done = f32[64,128]{1,0:T(8,128)} async-done(((f32[256,128]{1,0:T(8,128)}), f32[64,128]{1,0:T(8,128)}) %reduce-scatter.7.cloned.1.call-update) | async-done | bytes 32784 | tf_op jit(solution)/shard_map/reduce_scatter | solution.py:79
  79.9 0.8 fusion.19
  80.7 8.2 %all_gather.23 = bf16[256,128]{1,0:T(8,128)(2,1)S(1)} all-gather(bf16[64,128]{1,0:T(8,128)(2,1)S(1)} %fusion.19), channel_id=1, replica_groups=mesh['row'=4,'col'=8] {'row'}, dimensions={0}, use_global_device_ids=true | all-gather | bytes 81920 | tf_op jit(solution)/shard_map/all_gather | solution.py:72
  88.9 0.1 fusion.17
  89.0 24.0 %reduce-scatter.5.cloned.1.call-done = f32[64,128]{1,0:T(8,128)} async-done(((f32[512,128]{1,0:T(8,128)}), f32[64,128]{1,0:T(8,128)}) %reduce-scatter.5.cloned.1.call-update) | async-done | bytes 32784 | tf_op jit(solution)/shard_map/reduce_scatter | solution.py:76
  113.0 0.8 fusion.18
  113.8 13.9 %all_gather.22 = bf16[512,128]{1,0:T(8,128)(2,1)S(1)} all-gather(bf16[64,128]{1,0:T(8,128)(2,1)S(1)} %fusion.18), channel_id=1, replica_groups=mesh['row'=4,'col'=8] {'col'}, dimensions={0}, use_global_device_ids=true | all-gather | bytes 147456 | tf_op jit(solution)/shard_map/all_gather | solution.py:71
  127.7 0.1 fusion.15
  127.9 0.4 convert_reduce_fusion
  128.3 0.9 convolution_subtract_fusion.2
  129.3 0.9 convolution_subtract_fusion
  130.3 21.4 %reduce-scatter.11.cloned.1.call-done = f32[64,128]{1,0:T(8,128)} async-done(((f32[256,128]{1,0:T(8,128)}), f32[64,128]{1,0:T(8,128)}) %reduce-scatter.11.cloned.1.call-update) | async-done | bytes 32784 | tf_op jit(solution)/shard_map/reduce_scatter | solution.py:88
  151.6 1.4 broadcast_multiply_fusion
  153.0 31.5 %reduce-scatter.9.cloned.1.call-done = f32[64,128]{1,0:T(8,128)} async-done(((f32[512,128]{1,0:T(8,128)}), f32[64,128]{1,0:T(8,128)}) %reduce-scatter.9.cloned.1.call-update) | async-done | bytes 32784 | tf_op jit(solution)/shard_map/reduce_scatter | solution.py:85
  184.5 1.4 broadcast_multiply_fusion.1
  (21 shorter events, 0.4 us)
Async XLA Ops:
  7.2 16.0 %copy-start.4 = (bf16[64,128]{1,0:T(8,128)(2,1)S(1)}, bf16[64,128]{1,0:T(8,128)(2,1)}, u32[]{:S(2)}) copy-start(bf16[64,128]{1,0:T(8,128)(2,1)} %param.7) | copy-start | bytes 49156
  7.2 72.7 %reduce-scatter.7.cloned.1.call-start = ((), (), s32[]{:S(2)}) async-start(), calls=%async_computation.5 | async-start | bytes 163840 | tf_op jit(solution)/shard_map/reduce_scatter | solution.py:79
  23.2 8.4 %copy-start.1 = (f32[64,128]{1,0:T(8,128)S(1)}, f32[64,128]{1,0:T(8,128)}, u32[]{:S(2)}) copy-start(f32[64,128]{1,0:T(8,128)} %param.4) | copy-start | bytes 98308
  31.6 14.0 %copy-start = (f32[64,128]{1,0:T(8,128)S(1)}, f32[64,128]{1,0:T(8,128)}, u32[]{:S(2)}) copy-start(f32[64,128]{1,0:T(8,128)} %param.5) | copy-start | bytes 98308
  55.7 57.3 %reduce-scatter.5.cloned.1.call-start = ((), (), s32[]{:S(2)}) async-start(), calls=%async_computation.4 | async-start | bytes 294912 | tf_op jit(solution)/shard_map/reduce_scatter | solution.py:76
  56.7 94.9 %reduce-scatter.11.cloned.1.call-start = ((), (), s32[]{:S(2)}) async-start(), calls=%async_computation.7 | async-start | bytes 163840 | tf_op jit(solution)/shard_map/reduce_scatter | solution.py:88
  129.2 55.3 %reduce-scatter.9.cloned.1.call-start = ((), (), s32[]{:S(2)}) async-start(), calls=%async_computation.6 | async-start | bytes 294912 | tf_op jit(solution)/shard_map/reduce_scatter | solution.py:85
  130.2 21.4 %copy-start.2 = (f32[64,128]{1,0:T(8,128)S(1)}, f32[64,128]{1,0:T(8,128)}, u32[]{:S(2)}) copy-start(f32[64,128]{1,0:T(8,128)} %reduce-scatter.7.cloned.1.call-done) | copy-start | bytes 98308
  130.3 54.3 %copy-start.3 = (f32[64,128]{1,0:T(8,128)S(1)}, f32[64,128]{1,0:T(8,128)}, u32[]{:S(2)}) copy-start(f32[64,128]{1,0:T(8,128)} %reduce-scatter.5.cloned.1.call-done) | copy-start | bytes 98308
Sparse Core Ops, SparseCore 0:
  55.8 24.0 reduce-scatter.6
  82.1 30.8 reduce-scatter.4
  129.4 22.2 reduce-scatter.10
  153.7 30.7 reduce-scatter.8
where the time goes:
time: 193 us; the launch traced here: 192 us
  waiting for transfers between devices  100 us (52%)
  blocking collectives  68.7 us (36%)
  between operations  13.8 us (7%)
  other arithmetic  4.83 us (3%)
  matrix products  4.78 us (2%)
    reduce_scatter x2, waiting for transfers between devices, body(): lax.psum_scatter(left_term, 'col', scatter_dimension=0, tiled=True)  55.5 us
    reduce_scatter x2, waiting for transfers between devices, body(): lax.psum_scatter(right_term, 'row', scatter_dimension=0, tiled=True)  44.5 us
    all_gather x2, blocking collectives, body(): lax.all_gather(left_own.astype(jnp.bfloat16), 'col', axis=0, tiled=True)  28 us
    all_gather x2, blocking collectives, body(): lax.all_gather(right_own.astype(jnp.bfloat16), 'row', axis=0, tiled=True)  16.4 us
    all_gather x1, blocking collectives, body(): left_panel = lax.all_gather(left_cotangent, 'col', axis=0, tiled=True)  15.9 us
    all_gather x1, blocking collectives, body(): right_panel = lax.all_gather(right_coefficient, 'row', axis=0, tiled=True)  8.36 us
  transfers between devices with their start and end apart: 4, of which 4 were waited for; matrix products, arithmetic and copies ran while one was open for 2% of the time, Pallas kernels for 0%

commit v1 on v0

--- a/solution.py
+++ b/solution.py
@@ -1,7 +1,13 @@
+import functools
+import math
+
 import jax
 import jax.numpy as jnp
 from jax import lax
+from jax.experimental import pallas as pl
+from jax.experimental.pallas import tpu as pltpu
 from jax.sharding import PartitionSpec as P
+
 
 STEPS = 2
 
@@ -9,6 +15,15 @@
 inverse_width = 0.03125
 grad_scale = 0.0625
 descent_rate = 0.3
+
+
+f32 = jnp.float32
+bf16 = jnp.bfloat16
+exp2_scale = inverse_width * math.log2(math.e)
+step_scale = descent_rate * grad_scale
+LAST = (((1,), (1,)), ((), ()))
+FIRST = (((0,), (0,)), ((), ()))
+VMEM_BUDGET = 40 << 20
 
 
 def tile_terms(left_bf, left_panel, right_bf, right_panel):
@@ -60,7 +75,7 @@
     )
 
 
-def body(left_points, right_points, left_cotangent, right_coefficient):
+def partitioned_body(left_points, right_points, left_cotangent, right_coefficient):
     left_panel = lax.all_gather(left_cotangent, "col", axis=0, tiled=True)
     right_panel = lax.all_gather(right_coefficient, "row", axis=0, tiled=True)
     left_own = left_points
@@ -92,17 +107,335 @@
     return (left_own, right_own, left_grad, right_grad)
 
 
+def squares(wide):
+    square = wide * wide
+    high = square.astype(bf16)
+    return jnp.concatenate([high, (square - high.astype(f32)).astype(bf16)], axis=1)
+
+
+def norm_row(feat):
+    both = squares(feat.astype(f32))
+    return lax.dot_general(jnp.ones((8, both.shape[1]), bf16), both, LAST, preferred_element_type=f32)
+
+
+def norm_column(feat):
+    both = squares(feat.astype(f32))
+    return jnp.dot(both, jnp.ones((both.shape[1], feat.shape[1]), bf16), preferred_element_type=f32)
+
+
+def with_ones(feat):
+    return jnp.concatenate([feat, jnp.ones_like(feat)], axis=1)
+
+
+def rows_of(ref, side, kind):
+    blocks, both, width = ref.shape[1:]
+    points = both // 2
+    return ref[side, :, kind * points : (kind + 1) * points, :].reshape(blocks * points, width)
+
+
+def ones_rows(blocks, sets, side):
+    return jnp.concatenate([with_ones(rows_of(blocks[x], side, 0)) for x in sets], axis=0)
+
+
+def products(blocks, lefts, rights, place, left_norm, right_norm, product):
+    size, width = left_norm.shape[1:]
+    for m, left in enumerate(lefts):
+        feat, panel = rows_of(blocks[left], 0, 0), rows_of(blocks[left], 0, 1)
+        norm = jnp.concatenate([left_norm[place(left)]] * (size // width), axis=1)
+        for n, k in enumerate(rights):
+            crossed = lax.dot_general(feat, rows_of(blocks[k, 0], 1, 0), LAST, preferred_element_type=f32)
+            weight = lax.dot_general(panel, rows_of(blocks[k, 0], 1, 1), LAST, preferred_element_type=f32)
+            kernel = jnp.exp2((2.0 * exp2_scale) * crossed - norm - right_norm[k, 0:1, :])
+            product[m * size : (m + 1) * size, n * size : (n + 1) * size] = (weight * kernel).astype(bf16)
+
+
+def stage_kernel(plan, sets, *refs):
+    rects, new_left, new_right, fresh_left, fresh_right, first = plan
+    count = len(sets)
+    blocks = dict(zip(sets, refs[:count]))
+    state = refs[count + (0 if first else 4) : -1]
+    left_sum, right_sum, left_norm, right_norm = state
+    product = refs[-1]
+    fresh_left, fresh_right = set(fresh_left), set(fresh_right)
+
+    def place(left):
+        return left[1] * (left_sum.shape[0] // 2) + left[0]
+
+    for left in new_left:
+        left_norm[place(left)] = exp2_scale * norm_column(rows_of(blocks[left], 0, 0))
+    for k in new_right:
+        right_norm[k] = exp2_scale * norm_row(rows_of(blocks[k, 0], 1, 0))
+    for lefts, rights in rects:
+        products(blocks, lefts, rights, place, left_norm, right_norm, product)
+        others = ones_rows(blocks, [(k, 0) for k in rights], 1)
+        size = others.shape[0] // len(rights)
+        for m, left in enumerate(lefts):
+            term = jnp.dot(
+                product[m * size : (m + 1) * size, : len(rights) * size], others, preferred_element_type=f32
+            )
+            if left in fresh_left:
+                fresh_left.discard(left)
+                left_sum[place(left)] = term
+            else:
+                left_sum[place(left)] += term
+        others = ones_rows(blocks, lefts, 0)
+        for n, k in enumerate(rights):
+            term = lax.dot_general(
+                product[: len(lefts) * size, n * size : (n + 1) * size], others, FIRST, preferred_element_type=f32
+            )
+            if k in fresh_right:
+                fresh_right.discard(k)
+                right_sum[k] = term
+            else:
+                right_sum[k] += term
+
+
+def left_kernel(rows, points_left, left_sum, right_norm, *refs):
+    every, (sent, own, product, left_norm) = refs[: 2 * rows], refs[2 * rows :]
+    blocks = {(i % rows, i // rows): x for i, x in enumerate(every)}
+    last = (rows - 1, 1)
+    size, width = left_sum.shape[1], left_sum.shape[2] // 2
+    rights = list(range(rows))
+    left_norm[0] = exp2_scale * norm_column(rows_of(blocks[last], 0, 0))
+    products(blocks, [last], rights, lambda _: 0, left_norm, right_norm, product)
+    for index in range(2 * rows):
+        if index < 2 * rows - 1:
+            both = left_sum[index]
+        else:
+            both = jnp.dot(product[...], ones_rows(blocks, [(k, 0) for k in rights], 1), preferred_element_type=f32)
+        term = both[:, :width] - both[:, width:] * rows_of(every[index], 0, 0).astype(f32)
+        sent[index * size : (index + 1) * size, :] = term.astype(bf16)
+        if index == 0:
+            own[...] = points_left[...] - step_scale * term[: own.shape[0], :]
+
+
+def right_kernel(rows, points_right, right_sum, product, last, *refs):
+    near, (sent, own) = refs[:rows], refs[rows:]
+    size, width = right_sum.shape[1], right_sum.shape[2] // 2
+    others = with_ones(rows_of(last, 0, 0))
+    for index in range(rows):
+        both = right_sum[index] + lax.dot_general(
+            product[:, index * size : (index + 1) * size], others, FIRST, preferred_element_type=f32
+        )
+        wide = rows_of(near[index], 1, 0).astype(f32)
+        change = step_scale * (both[:, :width] - both[:, width:] * wide)
+        sent[index * size : (index + 1) * size, :] = (wide - change).astype(bf16)
+        if index == 0:
+            own[...] = points_right[...] - change[: own.shape[0], :]
+
+
+def own_weights_kernel(rows, *refs):
+    every, (left_weight, right_weight) = refs[: 2 * rows], refs[2 * rows :]
+    points = left_weight.shape[0]
+    size = left_weight.shape[1] // (2 * rows)
+    for side, out in ((0, left_weight), (1, right_weight)):
+        panel = every[0][side, 0, points:, :]
+        for index in range(2 * rows):
+            out[:, index * size : (index + 1) * size] = lax.dot_general(
+                panel, rows_of(every[index], 1 - side, 1), LAST, preferred_element_type=f32
+            )
+
+
+def own_term(feat, weight, others):
+    crossed = lax.dot_general(feat, others, LAST, preferred_element_type=f32)
+    wide = feat.astype(f32)
+    norm = jnp.sum(wide * wide, axis=1, keepdims=True)
+    other_norm = norm_row(others)[0:1, :]
+    kernel = jnp.exp2(exp2_scale * (2.0 * crossed - norm - other_norm))
+    product = (weight * kernel).astype(bf16)
+    total = jnp.sum(product.astype(f32), axis=1, keepdims=True)
+    return jnp.dot(product, others, preferred_element_type=f32) - total * wide
+
+
+def last_right_kernel(rows, sent, came, own, weight, *refs):
+    every, (new, grad, others) = refs[: 2 * rows], refs[2 * rows :]
+    half = sent.shape[0] // 2
+    size = half // rows
+    for index in range(2 * rows):
+        mine = index * size
+        theirs = (mine + half) % (2 * half)
+        change = sent[mine : mine + size, :].astype(f32) + came[theirs : theirs + size, :].astype(f32)
+        feat = rows_of(every[index], 0, 0).astype(f32) - step_scale * change
+        others[mine : mine + size, :] = feat.astype(bf16)
+    value = own[...]
+    term = grad_scale * own_term(value.astype(bf16), weight[...], others[...])
+    grad[...] = term
+    new[...] = value - descent_rate * term
+
+
+def last_left_kernel(left_came, sent, came, own, weight, right_new, right_grad, *refs):
+    outs, (others, new, grad, sems) = refs[:4], refs[4:]
+    copies = [
+        pltpu.make_async_copy(x, out, sems.at[i])
+        for i, (x, out) in enumerate(zip((right_new, right_grad, new, grad), (outs[1], outs[3], outs[0], outs[2])))
+    ]
+    copies[0].start()
+    copies[1].start()
+    points = own.shape[0]
+    half = sent.shape[0]
+    others[:half, :] = sent[...]
+    others[half:, :] = came[...]
+    value = own[...] - step_scale * left_came[half : half + points, :].astype(f32)
+    term = grad_scale * own_term(value.astype(bf16), weight[...], others[...])
+    grad[...] = term
+    new[...] = value - descent_rate * term
+    copies[2].start()
+    copies[3].start()
+    for copy in copies:
+        copy.wait()
+
+
+def pack_kernel(left, right, left_panel, right_panel, out, left_held, right_held, sems):
+    points = left.shape[0]
+    moves = ((left, left_held), (right, right_held), (left_panel, out.at[0, points:]), (right_panel, out.at[1, points:]))
+    copies = [pltpu.make_async_copy(source, target, sems.at[i]) for i, (source, target) in enumerate(moves)]
+    for copy in copies:
+        copy.start()
+    for copy in copies:
+        copy.wait()
+    out[0, :points, :] = left_held[...].astype(bf16)
+    out[1, :points, :] = right_held[...].astype(bf16)
+
+
+def call(kernel, inputs, outputs, scratch=(), aliases=None, flops=0, in_space=pltpu.VMEM, out_space=pltpu.VMEM, limit=VMEM_BUDGET):
+    moved = sum(x.size * x.dtype.itemsize for x in (*inputs, *outputs))
+    return pl.pallas_call(
+        kernel,
+        out_shape=tuple(outputs),
+        in_specs=[pl.BlockSpec(memory_space=in_space)] * len(inputs),
+        out_specs=(pl.BlockSpec(memory_space=out_space),) * len(outputs),
+        scratch_shapes=list(scratch),
+        input_output_aliases=aliases or {},
+        cost_estimate=pl.CostEstimate(flops=flops, bytes_accessed=moved // 8, transcendentals=0),
+        compiler_params=pltpu.CompilerParams(vmem_limit_bytes=limit),
+    )(*inputs)
+
+
+def replicated_body(rows, cols, left_points, right_points, left_cotangent, right_coefficient):
+    points, width = left_points.shape
+    pairs = cols // 2
+    size = pairs * points
+    shape = jax.ShapeDtypeStruct
+
+    def along_col(x, k):
+        return lax.ppermute(x, "col", [(i, (i + 2 * k) % cols) for i in range(cols)])
+
+    def along_row(x, k):
+        def target(i):
+            return i ^ k if rows & (rows - 1) == 0 else (i + k) % rows
+
+        return lax.ppermute(x, "row", [(i, target(i)) for i in range(rows)])
+
+    def partner(x):
+        return lax.ppermute(x, "col", [(i, i ^ 1) for i in range(cols)])
+
+    own_shape = shape((points, width), f32)
+    packed, left_held, right_held = call(
+        pack_kernel,
+        [pltpu.with_memory_space_constraint(x, pltpu.HBM) for x in (left_points, right_points, left_cotangent, right_coefficient)],
+        [shape((2, 2 * points, width), bf16), own_shape, own_shape],
+        [pltpu.SemaphoreType.DMA((4,))],
+        in_space=pl.ANY,
+    )
+    across = jnp.concatenate([along_col(packed, k) for k in range(1, pairs)], axis=1)
+    direct = [packed] + [along_row(packed, k) for k in range(1, rows)]
+    rest = [across] + [along_row(across, k) for k in range(1, rows)]
+    blocks = {}
+    for k in range(rows):
+        near = jnp.concatenate([direct[k], rest[k]], axis=1)
+        blocks[k, 0] = near.reshape(2, pairs, 2 * points, width)
+        blocks[k, 1] = partner(near).reshape(2, pairs, 2 * points, width)
+
+    state = (
+        shape((2 * rows, size, 2 * width), f32),
+        shape((rows, size, 2 * width), f32),
+        shape((2 * rows, size, width), f32),
+        shape((rows, 8, size), f32),
+    )
+    values = None
+    seen_left, seen_right = set(), set()
+
+    def stage(rects, new_left, new_right):
+        nonlocal values
+        sets = sorted({x for lefts, _ in rects for x in lefts} | {(k, 0) for _, rights in rects for k in rights})
+        lefts = {x for part, _ in rects for x in part}
+        rights = {k for _, part in rects for k in part}
+        plan = (rects, new_left, new_right, lefts - seen_left, rights - seen_right, values is None)
+        seen_left.update(lefts)
+        seen_right.update(rights)
+        inputs = [blocks[x] for x in sets] + list(values or ())
+        values = call(
+            functools.partial(stage_kernel, plan, sets),
+            inputs,
+            state,
+            [pltpu.VMEM((max(len(a) for a, _ in rects) * size, max(len(b) for _, b in rects) * size), bf16)],
+            aliases={len(sets) + i: i for i in range(4)} if values else None,
+            flops=sum(len(a) * len(b) for a, b in rects) * 12 * size * size * width,
+        )
+
+    waiting = []
+    for k in range(rows):
+        old = [(i, half) for half in (0, 1) for i in range(k) if (i, half) in seen_left]
+        rects = ([(old, [k])] if old else []) + [([(k, 0)], list(range(k + 1)))]
+        stage(rects, [(k, 0)], [k])
+        waiting.append((k, 1))
+        if k != 1 and k != rows - 1:
+            stage([(waiting, list(range(k + 1)))], waiting, [])
+            waiting = []
+    if waiting[:-1]:
+        stage([(waiting[:-1], list(range(rows)))], waiting[:-1], [])
+    left_sum, right_sum, _, right_norm = values
+    near = [blocks[k, 0] for k in range(rows)]
+    every = near + [blocks[k, 1] for k in range(rows)]
+    left_sent, left_own, product = call(
+        functools.partial(left_kernel, rows),
+        [left_held, left_sum, right_norm] + every,
+        [shape((2 * rows * size, width), bf16), own_shape, shape((size, rows * size), bf16)],
+        [pltpu.VMEM((1, size, width), f32)],
+    )
+    left_came = partner(left_sent)
+    right_sent, right_own = call(
+        functools.partial(right_kernel, rows),
+        [right_held, right_sum, product, blocks[rows - 1, 1]] + near,
+        [shape((rows * size, width), bf16), own_shape],
+    )
+    right_came = partner(right_sent)
+    left_weight, right_weight = call(
+        functools.partial(own_weights_kernel, rows), every, [shape((points, 2 * rows * size), f32)] * 2
+    )
+    scratch = [pltpu.VMEM((2 * rows * size, width), bf16)]
+    right_new, right_grad = call(
+        functools.partial(last_right_kernel, rows),
+        [left_sent, left_came, right_own, right_weight] + every,
+        [own_shape] * 2,
+        scratch,
+    )
+    return call(
+        last_left_kernel,
+        [left_came, right_sent, right_came, left_own, left_weight, right_new, right_grad],
+        [own_shape] * 4,
+        scratch + [pltpu.VMEM((points, width), f32)] * 2 + [pltpu.SemaphoreType.DMA((4,))],
+        out_space=pltpu.HBM,
+    )
+
+
+def replicated(rows, cols, shapes):
+    points, width = shapes[0]
+    total = rows * cols * points
+    held = total * total + 24 * total * width
+    size = cols // 2 * points
+    even = cols % 2 == 0 and width % 128 == 0 and size % width == 0 and rows > 2 and cols > 2
+    return STEPS == 2 and even and len(set(shapes)) == 1 and held <= VMEM_BUDGET // 2
+
+
+def body(rows, cols, *arrays):
+    if replicated(rows, cols, [x.shape for x in arrays]):
+        return replicated_body(rows, cols, *arrays)
+    return partitioned_body(*arrays)
+
+
 def solution(mesh):
-    in_specs = (
-        P(("row", "col"), None),
-        P(("row", "col"), None),
-        P(("row", "col"), None),
-        P(("row", "col"), None),
-    )
-    out_specs = (
-        P(("row", "col"), None),
-        P(("row", "col"), None),
-        P(("row", "col"), None),
-        P(("row", "col"), None),
-    )
-    return jax.shard_map(body, mesh=mesh, in_specs=in_specs, out_specs=out_specs, check_vma=False)
+    spec = P(("row", "col"), None)
+    rows, cols = mesh.shape["row"], mesh.shape["col"]
+    run = functools.partial(body, rows, cols)
+    return jax.shard_map(run, mesh=mesh, in_specs=(spec,) * 4, out_specs=(spec,) * 4, check_vma=False)

time: 193 us -> 35.7 us (0.18)
  waiting for transfers between devices: 100 us -> 8.63 us
  blocking collectives: 68.7 us -> 0 us
  starting transfers between devices: 0.16 us -> 15.6 us
  between operations: 13.8 us -> 0.86 us
  Pallas kernels: 0 us -> 10.3 us
  other arithmetic: 4.83 us -> 0 us
  matrix products: 4.78 us -> 0 us
    reduce_scatter x4 -> x0, waiting for transfers between devices: 100 us -> none  [the longest x2 55.5 us: body(): lax.psum_scatter(left_term, 'col', scatter_dimension=0, tiled=True)]
    all_gather x6 -> x0, blocking collectives: 68.7 us -> none  [the longest x2 28 us: body(): lax.all_gather(left_own.astype(jnp.bfloat16), 'col', axis=0, tiled=True)]
    ppermute x0 -> x15, starting transfers between devices: none -> 15.6 us  [the longest x6 7.11 us: along_row(): return lax.ppermute(x, 'row', [(i, target(i)) for i in range(rows)])]
    pallas_call x0 -> x12, Pallas kernels: none -> 10.3 us  [call(): pl.pallas_call(kernel, out_shape=tuple(outputs), in_specs=[pl.BlockSpec(m...]
    ppermute x0 -> x15, waiting for transfers between devices: none -> 8.63 us  [the longest x6 8.12 us: along_row(): return lax.ppermute(x, 'row', [(i, target(i)) for i in range(rows)])]
    dot_general x7 -> x0, matrix products: 4.78 us -> none  [the longest x2 1.87 us: visit_block(): jnp.dot(product, right_bf, preferred_element_type=jnp.float32)]
    mul x2 -> x0, other arithmetic: 2.77 us -> none  [the longest x1 1.39 us: body(): lax.psum_scatter(right_term, 'row', scatter_dimension=0, tiled=True)]
  transfers between devices with their start and end apart: 4 -> 15, of which waited for: 4 -> 3; matrix products, arithmetic and copies ran while one was open for 2% -> 1% of each run, Pallas kernels for 0% -> 21%
where the time goes in v1:
time: 35.7 us; the launch traced here: 35.5 us
  starting transfers between devices  15.6 us (44%)
  Pallas kernels  10.3 us (29%)
  waiting for transfers between devices  8.63 us (24%)
  between operations  0.86 us (2%)
    pallas_call x12, Pallas kernels, call(): pl.pallas_call(kernel, out_shape=tuple(outputs), in_specs=[pl.BlockSpec(m...  10.3 us
    ppermute x6, waiting for transfers between devices, along_row(): return lax.ppermute(x, 'row', [(i, target(i)) for i in range(rows)])  8.12 us
    ppermute x6, starting transfers between devices, along_row(): return lax.ppermute(x, 'row', [(i, target(i)) for i in range(rows)])  7.11 us
    ppermute x3, starting transfers between devices, along_col(): lax.ppermute(x, 'col', [(i, (i + 2 * k) % cols) for i in range(cols)])  7.04 us
    ppermute x6, starting transfers between devices, partner(): return lax.ppermute(x, 'col', [(i, i ^ 1) for i in range(cols)])  1.41 us
  transfers between devices with their start and end apart: 15, of which 3 were waited for; matrix products, arithmetic and copies ran while one was open for 1% of the time, Pallas kernels for 21%

profile of v1, /device:TPU:0, one launch (start us, length us, event | category | flops | bytes accessed | tf_op | source)
XLA Modules:
  0.0 35.5 jit_solution(15669389227732761410)
XLA Ops:
  0.6 0.8 %shard_map.75 = (bf16[2,128,128]{2,1,0:T(8,128)(2,1)S(1)}, f32[64,128]{1,0:T(8,128)S(1)}, f32[64,128]{1,0:T(8,128)S(1)}) custom-call(f32[64,128]{1,0:T(8,128)} %left.1, f32[64,128]{1,0:T(8,128)} %right.1, bf16[64,128]{1,0:T(8,128)(2,1)} %left_panel.1, bf16[64,128]{1,0:T(8,128)(2,1)} %right_panel.1), custom_call_target="tpu_custom_call" | custom-call | bytes 28672 | tf_op jit(solution)/shard_map/pallas_call | solution.py:302
  1.5 3.1 %collective-permute-start = (bf16[2,128,128]{2,1,0:T(8,128)(2,1)S(1)}, bf16[2,128,128]{2,1,0:T(8,128)(2,1)S(1)}, u32[]{:S(2)}, u32[]{:S(2)}) collective-permute-start(bf16[2,128,128]{2,1,0:T(8,128)(2,1)S(1)} %get-tuple-element.40), channel_id=1, source_target_pairs={{0,2},{1,3},{2,4},{3,5},{4,6},{5,7},{6,0},{7,1},{8,10},{9,11},{10,... | collective-permute-start | bytes 196616 | tf_op jit(solution)/shard_map/ppermute | solution.py:321
  4.6 2.6 %collective-permute-start.1 = (bf16[2,128,128]{2,1,0:T(8,128)(2,1)S(1)}, bf16[2,128,128]{2,1,0:T(8,128)(2,1)S(1)}, u32[]{:S(2)}, u32[]{:S(2)}) collective-permute-start(bf16[2,128,128]{2,1,0:T(8,128)(2,1)S(1)} %get-tuple-element.40), channel_id=1, source_target_pairs={{0,4},{1,5},{2,6},{3,7},{4,0},{5,1},{6,2},{7,3},{8,12},{9,13},{10,... | collective-permute-start | bytes 196616 | tf_op jit(solution)/shard_map/ppermute | solution.py:321
  7.2 1.3 %collective-permute-start.2 = (bf16[2,128,128]{2,1,0:T(8,128)(2,1)S(1)}, bf16[2,128,128]{2,1,0:T(8,128)(2,1)S(1)}, u32[]{:S(2)}, u32[]{:S(2)}) collective-permute-start(bf16[2,128,128]{2,1,0:T(8,128)(2,1)S(1)} %get-tuple-element.40), channel_id=1, source_target_pairs={{0,6},{1,7},{2,0},{3,1},{4,2},{5,3},{6,4},{7,5},{8,14},{9,15},{10,... | collective-permute-start | bytes 196616 | tf_op jit(solution)/shard_map/ppermute | solution.py:321
  8.5 1.5 %collective-permute-start.4 = (bf16[2,128,128]{2,1,0:T(8,128)(2,1)S(1)}, bf16[2,128,128]{2,1,0:T(8,128)(2,1)S(1)}, u32[]{:S(2)}, u32[]{:S(2)}) collective-permute-start(bf16[2,128,128]{2,1,0:T(8,128)(2,1)S(1)} %get-tuple-element.40), channel_id=1, source_target_pairs={{0,8},{8,0},{16,24},{24,16},{1,9},{9,1},{17,25},{25,17},{2,10},{10... | collective-permute-start | bytes 196616 | tf_op jit(solution)/shard_map/ppermute | solution.py:327
  10.0 1.5 %collective-permute-start.7 = (bf16[2,128,128]{2,1,0:T(8,128)(2,1)S(1)}, bf16[2,128,128]{2,1,0:T(8,128)(2,1)S(1)}, u32[]{:S(2)}, u32[]{:S(2)}) collective-permute-start(bf16[2,128,128]{2,1,0:T(8,128)(2,1)S(1)} %get-tuple-element.40), channel_id=1, source_target_pairs={{0,16},{8,24},{16,0},{24,8},{1,17},{9,25},{17,1},{25,9},{2,18},{10... | collective-permute-start | bytes 196616 | tf_op jit(solution)/shard_map/ppermute | solution.py:327
  11.5 0.5 %collective-permute-start.10 = (bf16[2,128,128]{2,1,0:T(8,128)(2,1)S(1)}, bf16[2,128,128]{2,1,0:T(8,128)(2,1)S(1)}, u32[]{:S(2)}, u32[]{:S(2)}) collective-permute-start(bf16[2,128,128]{2,1,0:T(8,128)(2,1)S(1)} %get-tuple-element.40), channel_id=1, source_target_pairs={{0,24},{8,16},{16,8},{24,0},{1,25},{9,17},{17,9},{25,1},{2,26},{10... | collective-permute-start | bytes 196616 | tf_op jit(solution)/shard_map/ppermute | solution.py:327
  12.2 1.6 %collective-permute-start.5 = (bf16[2,384,128]{2,1,0:T(8,128)(2,1)S(1)}, bf16[2,384,128]{2,1,0:T(8,128)(2,1)S(1)}, u32[]{:S(2)}, u32[]{:S(2)}) collective-permute-start(bf16[2,384,128]{2,1,0:T(8,128)(2,1)S(1)} %get-tuple-element.74), channel_id=1, source_target_pairs={{0,8},{8,0},{16,24},{24,16},{1,9},{9,1},{17,25},{25,17},{2,10},{10... | collective-permute-start | bytes 589832 | tf_op jit(solution)/shard_map/ppermute | solution.py:327
  13.7 1.5 %collective-permute-start.8 = (bf16[2,384,128]{2,1,0:T(8,128)(2,1)S(1)}, bf16[2,384,128]{2,1,0:T(8,128)(2,1)S(1)}, u32[]{:S(2)}, u32[]{:S(2)}) collective-permute-start(bf16[2,384,128]{2,1,0:T(8,128)(2,1)S(1)} %get-tuple-element.74), channel_id=1, source_target_pairs={{0,16},{8,24},{16,0},{24,8},{1,17},{9,25},{17,1},{25,9},{2,18},{10... | collective-permute-start | bytes 589832 | tf_op jit(solution)/shard_map/ppermute | solution.py:327
  15.3 0.5 %collective-permute-start.11 = (bf16[2,384,128]{2,1,0:T(8,128)(2,1)S(1)}, bf16[2,384,128]{2,1,0:T(8,128)(2,1)S(1)}, u32[]{:S(2)}, u32[]{:S(2)}) collective-permute-start(bf16[2,384,128]{2,1,0:T(8,128)(2,1)S(1)} %get-tuple-element.74), channel_id=1, source_target_pairs={{0,24},{8,16},{16,8},{24,0},{1,25},{9,17},{17,9},{25,1},{2,26},{10... | collective-permute-start | bytes 589832 | tf_op jit(solution)/shard_map/ppermute | solution.py:327
  15.8 4.9 %collective-permute-done.5 = bf16[2,384,128]{2,1,0:T(8,128)(2,1)S(1)} collective-permute-done((bf16[2,384,128]{2,1,0:T(8,128)(2,1)S(1)}, bf16[2,384,128]{2,1,0:T(8,128)(2,1)S(1)}, u32[]{:S(2)}, u32[]{:S(2)}) %collective-permute-start.5) | collective-permute-done | bytes 196640 | tf_op jit(solution)/shard_map/ppermute | solution.py:327
  20.8 3.2 %collective-permute-done.8 = bf16[2,384,128]{2,1,0:T(8,128)(2,1)S(1)} collective-permute-done((bf16[2,384,128]{2,1,0:T(8,128)(2,1)S(1)}, bf16[2,384,128]{2,1,0:T(8,128)(2,1)S(1)}, u32[]{:S(2)}, u32[]{:S(2)}) %collective-permute-start.8) | collective-permute-done | bytes 196640 | tf_op jit(solution)/shard_map/ppermute | solution.py:327
  24.2 0.5 %collective-permute-start.12 = (bf16[2,512,128]{2,1,0:T(8,128)(2,1)S(1)}, bf16[2,512,128]{2,1,0:T(8,128)(2,1)S(1)}, u32[]{:S(2)}, u32[]{:S(2)}) collective-permute-start(bf16[2,512,128]{2,1,0:T(8,128)(2,1)S(1)} %constant_dynamic-update-slice_fusion.11), channel_id=1, source_target_pairs={{0,1},{1,0},{2,3},{3,2},{4,5},{5,4},{6,7},{7,6},{8,9},{9,8},{10,11... | collective-permute-start | bytes 786440 | tf_op jit(solution)/shard_map/ppermute | solution.py:330
  24.8 0.5 %shard_map.76 = (f32[8,256,256]{2,1,0:T(8,128)S(1)}, f32[4,256,256]{2,1,0:T(8,128)S(1)}, f32[8,256,128]{2,1,0:T(8,128)S(1)}, f32[4,8,256]{2,1,0:T(8,128)S(1)}) custom-call(bf16[2,4,128,128]{3,2,1,0:T(8,128)(2,1)S(1)} %bitcast.8), custom_call_target="tpu_custom_call" | custom-call | flops 100663296 | bytes 561152 | tf_op jit(solution)/shard_map/pallas_call | solution.py:302
  25.3 0.5 %shard_map.77 = (f32[8,256,256]{2,1,0:T(8,128)S(1)}, f32[4,256,256]{2,1,0:T(8,128)S(1)}, f32[8,256,128]{2,1,0:T(8,128)S(1)}, f32[4,8,256]{2,1,0:T(8,128)S(1)}) custom-call(bf16[2,4,128,128]{3,2,1,0:T(8,128)(2,1)S(1)} %bitcast.9, bf16[2,4,128,128]{3,2,1,0:T(8,128)(2,1)S(1)} %bitcast.33, ...), custom_call_target="tpu_custom_call", output_to_operand_aliasing={{0}: (2, {}), {1}: (3, {}), {2}: (4, {}), {3}: (5, {})} | custom-call | flops 100663296 | bytes 1122304 | tf_op jit(solution)/shard_map/pallas_call | solution.py:302
  25.8 0.9 %shard_map.78 = (f32[8,256,256]{2,1,0:T(8,128)S(1)}, f32[4,256,256]{2,1,0:T(8,128)S(1)}, f32[8,256,128]{2,1,0:T(8,128)S(1)}, f32[4,8,256]{2,1,0:T(8,128)S(1)}) custom-call(bf16[2,4,128,128]{3,2,1,0:T(8,128)(2,1)S(1)} %bitcast.10, bf16[2,4,128,128]{3,2,1,0:T(8,128)(2,1)S(1)} %bitcast.34, ...), custom_call_target="tpu_custom_call", output_to_operand_aliasing={{0}: (3, {}), {1}: (4, {}), {2}: (5, {}), {3}: (6, {})} | custom-call | flops 402653184 | bytes 1155072 | tf_op jit(solution)/shard_map/pallas_call | solution.py:302
  26.7 1.1 %shard_map.79 = (f32[8,256,256]{2,1,0:T(8,128)S(1)}, f32[4,256,256]{2,1,0:T(8,128)S(1)}, f32[8,256,128]{2,1,0:T(8,128)S(1)}, f32[4,8,256]{2,1,0:T(8,128)S(1)}) custom-call(bf16[2,4,128,128]{3,2,1,0:T(8,128)(2,1)S(1)} %bitcast.11, bf16[2,4,128,128]{3,2,1,0:T(8,128)(2,1)S(1)} %bitcast.35, ...), custom_call_target="tpu_custom_call", output_to_operand_aliasing={{0}: (4, {}), {1}: (5, {}), {2}: (6, {}), {3}: (7, {})} | custom-call | flops 603979776 | bytes 1187840 | tf_op jit(solution)/shard_map/pallas_call | solution.py:302
  27.8 1.0 %shard_map.80 = (f32[8,256,256]{2,1,0:T(8,128)S(1)}, f32[4,256,256]{2,1,0:T(8,128)S(1)}, f32[8,256,128]{2,1,0:T(8,128)S(1)}, f32[4,8,256]{2,1,0:T(8,128)S(1)}) custom-call(bf16[2,4,128,128]{3,2,1,0:T(8,128)(2,1)S(1)} %bitcast.12, bf16[2,4,128,128]{3,2,1,0:T(8,128)(2,1)S(1)} %bitcast.20, ...), custom_call_target="tpu_custom_call", output_to_operand_aliasing={{0}: (5, {}), {1}: (6, {}), {2}: (7, {}), {3}: (8, {})} | custom-call | flops 603979776 | bytes 1220608 | tf_op jit(solution)/shard_map/pallas_call | solution.py:302
  28.9 1.6 %shard_map.81 = (f32[8,256,256]{2,1,0:T(8,128)S(1)}, f32[4,256,256]{2,1,0:T(8,128)S(1)}, f32[8,256,128]{2,1,0:T(8,128)S(1)}, f32[4,8,256]{2,1,0:T(8,128)S(1)}) custom-call(bf16[2,4,128,128]{3,2,1,0:T(8,128)(2,1)S(1)} %bitcast.13, bf16[2,4,128,128]{3,2,1,0:T(8,128)(2,1)S(1)} %bitcast.36, ...), custom_call_target="tpu_custom_call", output_to_operand_aliasing={{0}: (7, {}), {1}: (8, {}), {2}: (9, {}), {3}: (10, {})} | custom-call | flops 1006632960 | bytes 1286144 | tf_op jit(solution)/shard_map/pallas_call | solution.py:302
  30.5 0.7 %shard_map.82 = (bf16[2048,128]{1,0:T(8,128)(2,1)S(1)}, f32[64,128]{1,0:T(8,128)S(1)}, bf16[256,1024]{1,0:T(8,128)(2,1)S(1)}) custom-call(f32[64,128]{1,0:T(8,128)S(1)} %get-tuple-element.39.points_left, f32[8,256,256]{2,1,0:T(8,128)S(1)} %get-tuple-element.61.left_sum, f32[4,8,256]{2,1,0:T(8,128)S(1)} %get-tuple-element.62.right_norm, ...), custom_call_target="tpu_custom_call" | custom-call | bytes 667648 | tf_op jit(solution)/shard_map/pallas_call | solution.py:302
  31.6 0.6 %collective-permute-start.14 = (bf16[1024,128]{1,0:T(8,128)(2,1)S(1)}, bf16[1024,128]{1,0:T(8,128)(2,1)S(1)}, u32[]{:S(2)}, u32[]{:S(2)}) collective-permute-start(bf16[1024,128]{1,0:T(8,128)(2,1)S(1)} %get-tuple-element.67.sent), channel_id=1, source_target_pairs={{0,1},{1,0},{2,3},{3,2},{4,5},{5,4},{6,7},{7,6},{8,9},{9,8},{10,11... | collective-permute-start | bytes 786440 | tf_op jit(solution)/shard_map/ppermute | solution.py:330
  32.7 0.5 %collective-permute-done.13.came.left_came = bf16[2048,128]{1,0:T(8,128)(2,1)S(1)} collective-permute-done((bf16[2048,128]{1,0:T(8,128)(2,1)S(1)}, bf16[2048,128]{1,0:T(8,128)(2,1)S(1)}, u32[]{:S(2)}, u32[]{:S(2)}) %collective-permute-start.13) | collective-permute-done | bytes 524320 | tf_op jit(solution)/shard_map/ppermute | solution.py:330
  33.1 0.9 %shard_map.85 = (f32[64,128]{1,0:T(8,128)S(1)}, f32[64,128]{1,0:T(8,128)S(1)}) custom-call(bf16[2048,128]{1,0:T(8,128)(2,1)S(1)} %get-tuple-element.63.sent, bf16[2048,128]{1,0:T(8,128)(2,1)S(1)} %collective-permute-done.13.came.left_came, f32[64,128]{1,0:T(8,128)S(1)} %get-tuple-element.70.own, f32[64,2048]{1,0:T(8,128)S(1)} %get-tuple-element.71.weight, ...), custom_call_target="tpu_custom_call" | custom-call | bytes 471040 | tf_op jit(solution)/shard_map/pallas_call | solution.py:302
  34.1 1.4 %shard_map.86 = (f32[64,128]{1,0:T(8,128)}, f32[64,128]{1,0:T(8,128)}, f32[64,128]{1,0:T(8,128)}, f32[64,128]{1,0:T(8,128)}) custom-call(bf16[2048,128]{1,0:T(8,128)(2,1)S(1)} %collective-permute-done.13.came.left_came, bf16[1024,128]{1,0:T(8,128)(2,1)S(1)} %get-tuple-element.67.sent, bf16[1024,128]{1,0:T(8,128)(2,1)S(1)} %collective-permute-done.14.came, ...), custom_call_target="tpu_custom_call" | custom-call | bytes 225280 | tf_op jit(solution)/shard_map/pallas_call | solution.py:302
  (28 shorter events, 1.3 us)
Async XLA Ops:
  1.5 10.1 %collective-permute-start = (bf16[2,128,128]{2,1,0:T(8,128)(2,1)S(1)}, bf16[2,128,128]{2,1,0:T(8,128)(2,1)S(1)}, u32[]{:S(2)}, u32[]{:S(2)}) collective-permute-start(bf16[2,128,128]{2,1,0:T(8,128)(2,1)S(1)} %get-tuple-element.40), channel_id=1, source_target_pairs={{0,2},{1,3},{2,4},{3,5},{4,6},{5,7},{6,0},{7,1},{8,10},{9,11},{10,... | collective-permute-start | bytes 196616 | tf_op jit(solution)/shard_map/ppermute | solution.py:321
  4.6 7.5 %collective-permute-start.1 = (bf16[2,128,128]{2,1,0:T(8,128)(2,1)S(1)}, bf16[2,128,128]{2,1,0:T(8,128)(2,1)S(1)}, u32[]{:S(2)}, u32[]{:S(2)}) collective-permute-start(bf16[2,128,128]{2,1,0:T(8,128)(2,1)S(1)} %get-tuple-element.40), channel_id=1, source_target_pairs={{0,4},{1,5},{2,6},{3,7},{4,0},{5,1},{6,2},{7,3},{8,12},{9,13},{10,... | collective-permute-start | bytes 196616 | tf_op jit(solution)/shard_map/ppermute | solution.py:321
  7.2 5.0 %collective-permute-start.2 = (bf16[2,128,128]{2,1,0:T(8,128)(2,1)S(1)}, bf16[2,128,128]{2,1,0:T(8,128)(2,1)S(1)}, u32[]{:S(2)}, u32[]{:S(2)}) collective-permute-start(bf16[2,128,128]{2,1,0:T(8,128)(2,1)S(1)} %get-tuple-element.40), channel_id=1, source_target_pairs={{0,6},{1,7},{2,0},{3,1},{4,2},{5,3},{6,4},{7,5},{8,14},{9,15},{10,... | collective-permute-start | bytes 196616 | tf_op jit(solution)/shard_map/ppermute | solution.py:321
  8.5 6.8 %collective-permute-start.4 = (bf16[2,128,128]{2,1,0:T(8,128)(2,1)S(1)}, bf16[2,128,128]{2,1,0:T(8,128)(2,1)S(1)}, u32[]{:S(2)}, u32[]{:S(2)}) collective-permute-start(bf16[2,128,128]{2,1,0:T(8,128)(2,1)S(1)} %get-tuple-element.40), channel_id=1, source_target_pairs={{0,8},{8,0},{16,24},{24,16},{1,9},{9,1},{17,25},{25,17},{2,10},{10... | collective-permute-start | bytes 196616 | tf_op jit(solution)/shard_map/ppermute | solution.py:327
  10.0 5.8 %collective-permute-start.7 = (bf16[2,128,128]{2,1,0:T(8,128)(2,1)S(1)}, bf16[2,128,128]{2,1,0:T(8,128)(2,1)S(1)}, u32[]{:S(2)}, u32[]{:S(2)}) collective-permute-start(bf16[2,128,128]{2,1,0:T(8,128)(2,1)S(1)} %get-tuple-element.40), channel_id=1, source_target_pairs={{0,16},{8,24},{16,0},{24,8},{1,17},{9,25},{17,1},{25,9},{2,18},{10... | collective-permute-start | bytes 196616 | tf_op jit(solution)/shard_map/ppermute | solution.py:327
  11.5 12.7 %collective-permute-start.10 = (bf16[2,128,128]{2,1,0:T(8,128)(2,1)S(1)}, bf16[2,128,128]{2,1,0:T(8,128)(2,1)S(1)}, u32[]{:S(2)}, u32[]{:S(2)}) collective-permute-start(bf16[2,128,128]{2,1,0:T(8,128)(2,1)S(1)} %get-tuple-element.40), channel_id=1, source_target_pairs={{0,24},{8,16},{16,8},{24,0},{1,25},{9,17},{17,9},{25,1},{2,26},{10... | collective-permute-start | bytes 196616 | tf_op jit(solution)/shard_map/ppermute | solution.py:327
  12.2 8.5 %collective-permute-start.5 = (bf16[2,384,128]{2,1,0:T(8,128)(2,1)S(1)}, bf16[2,384,128]{2,1,0:T(8,128)(2,1)S(1)}, u32[]{:S(2)}, u32[]{:S(2)}) collective-permute-start(bf16[2,384,128]{2,1,0:T(8,128)(2,1)S(1)} %get-tuple-element.74), channel_id=1, source_target_pairs={{0,8},{8,0},{16,24},{24,16},{1,9},{9,1},{17,25},{25,17},{2,10},{10... | collective-permute-start | bytes 589832 | tf_op jit(solution)/shard_map/ppermute | solution.py:327
  13.7 10.3 %collective-permute-start.8 = (bf16[2,384,128]{2,1,0:T(8,128)(2,1)S(1)}, bf16[2,384,128]{2,1,0:T(8,128)(2,1)S(1)}, u32[]{:S(2)}, u32[]{:S(2)}) collective-permute-start(bf16[2,384,128]{2,1,0:T(8,128)(2,1)S(1)} %get-tuple-element.74), channel_id=1, source_target_pairs={{0,16},{8,24},{16,0},{24,8},{1,17},{9,25},{17,1},{25,9},{2,18},{10... | collective-permute-start | bytes 589832 | tf_op jit(solution)/shard_map/ppermute | solution.py:327
  15.3 8.9 %collective-permute-start.11 = (bf16[2,384,128]{2,1,0:T(8,128)(2,1)S(1)}, bf16[2,384,128]{2,1,0:T(8,128)(2,1)S(1)}, u32[]{:S(2)}, u32[]{:S(2)}) collective-permute-start(bf16[2,384,128]{2,1,0:T(8,128)(2,1)S(1)} %get-tuple-element.74), channel_id=1, source_target_pairs={{0,24},{8,16},{16,8},{24,0},{1,25},{9,17},{17,9},{25,1},{2,26},{10... | collective-permute-start | bytes 589832 | tf_op jit(solution)/shard_map/ppermute | solution.py:327
  15.8 9.6 %collective-permute-start.3 = (bf16[2,512,128]{2,1,0:T(8,128)(2,1)S(1)}, bf16[2,512,128]{2,1,0:T(8,128)(2,1)S(1)}, u32[]{:S(2)}, u32[]{:S(2)}) collective-permute-start(bf16[2,512,128]{2,1,0:T(8,128)(2,1)S(1)} %get-tuple-element.75), channel_id=1, source_target_pairs={{0,1},{1,0},{2,3},{3,2},{4,5},{5,4},{6,7},{7,6},{8,9},{9,8},{10,11... | collective-permute-start | bytes 786440 | tf_op jit(solution)/shard_map/ppermute | solution.py:330
  20.7 7.1 %collective-permute-start.6 = (bf16[2,512,128]{2,1,0:T(8,128)(2,1)S(1)}, bf16[2,512,128]{2,1,0:T(8,128)(2,1)S(1)}, u32[]{:S(2)}, u32[]{:S(2)}) collective-permute-start(bf16[2,512,128]{2,1,0:T(8,128)(2,1)S(1)} %constant_dynamic-update-slice_fusion.7), channel_id=1, source_target_pairs={{0,1},{1,0},{2,3},{3,2},{4,5},{5,4},{6,7},{7,6},{8,9},{9,8},{10,11... | collective-permute-start | bytes 786440 | tf_op jit(solution)/shard_map/ppermute | solution.py:330
  24.1 3.7 %collective-permute-start.9 = (bf16[2,512,128]{2,1,0:T(8,128)(2,1)S(1)}, bf16[2,512,128]{2,1,0:T(8,128)(2,1)S(1)}, u32[]{:S(2)}, u32[]{:S(2)}) collective-permute-start(bf16[2,512,128]{2,1,0:T(8,128)(2,1)S(1)} %constant_dynamic-update-slice_fusion.9), channel_id=1, source_target_pairs={{0,1},{1,0},{2,3},{3,2},{4,5},{5,4},{6,7},{7,6},{8,9},{9,8},{10,11... | collective-permute-start | bytes 786440 | tf_op jit(solution)/shard_map/ppermute | solution.py:330
  24.2 6.2 %collective-permute-start.12 = (bf16[2,512,128]{2,1,0:T(8,128)(2,1)S(1)}, bf16[2,512,128]{2,1,0:T(8,128)(2,1)S(1)}, u32[]{:S(2)}, u32[]{:S(2)}) collective-permute-start(bf16[2,512,128]{2,1,0:T(8,128)(2,1)S(1)} %constant_dynamic-update-slice_fusion.11), channel_id=1, source_target_pairs={{0,1},{1,0},{2,3},{3,2},{4,5},{5,4},{6,7},{7,6},{8,9},{9,8},{10,11... | collective-permute-start | bytes 786440 | tf_op jit(solution)/shard_map/ppermute | solution.py:330
  31.2 2.0 %collective-permute-start.13 = (bf16[2048,128]{1,0:T(8,128)(2,1)S(1)}, bf16[2048,128]{1,0:T(8,128)(2,1)S(1)}, u32[]{:S(2)}, u32[]{:S(2)}) collective-permute-start(bf16[2048,128]{1,0:T(8,128)(2,1)S(1)} %get-tuple-element.63.sent), channel_id=1, source_target_pairs={{0,1},{1,0},{2,3},{3,2},{4,5},{5,4},{6,7},{7,6},{8,9},{9,8},{10,11... | collective-permute-start | bytes 1572872 | tf_op jit(solution)/shard_map/ppermute | solution.py:330
  31.6 2.4 %collective-permute-start.14 = (bf16[1024,128]{1,0:T(8,128)(2,1)S(1)}, bf16[1024,128]{1,0:T(8,128)(2,1)S(1)}, u32[]{:S(2)}, u32[]{:S(2)}) collective-permute-start(bf16[1024,128]{1,0:T(8,128)(2,1)S(1)} %get-tuple-element.67.sent), channel_id=1, source_target_pairs={{0,1},{1,0},{2,3},{3,2},{4,5},{5,4},{6,7},{7,6},{8,9},{9,8},{10,11... | collective-permute-start | bytes 786440 | tf_op jit(solution)/shard_map/ppermute | solution.py:330

commit v2 on v1

--- a/solution.py
+++ b/solution.py
@@ -150,12 +150,11 @@
 
 
 def stage_kernel(plan, sets, *refs):
-    rects, new_left, new_right, fresh_left, fresh_right, first = plan
+    rects, new_left, new_right, fresh_left, fresh_right, first, keep = plan
     count = len(sets)
     blocks = dict(zip(sets, refs[:count]))
-    state = refs[count + (0 if first else 4) : -1]
-    left_sum, right_sum, left_norm, right_norm = state
-    product = refs[-1]
+    outs = refs[count + (0 if first else 4) :]
+    left_sum, right_sum, left_norm, right_norm = outs[:4]
     fresh_left, fresh_right = set(fresh_left), set(fresh_right)
 
     def place(left):
@@ -165,7 +164,8 @@
         left_norm[place(left)] = exp2_scale * norm_column(rows_of(blocks[left], 0, 0))
     for k in new_right:
         right_norm[k] = exp2_scale * norm_row(rows_of(blocks[k, 0], 1, 0))
-    for lefts, rights in rects:
+    for index, (lefts, rights) in enumerate(rects):
+        product = outs[4 + index] if keep else outs[4]
         products(blocks, lefts, rights, place, left_norm, right_norm, product)
         others = ones_rows(blocks, [(k, 0) for k in rights], 1)
         size = others.shape[0] // len(rights)
@@ -178,6 +178,8 @@
                 left_sum[place(left)] = term
             else:
                 left_sum[place(left)] += term
+        if keep:
+            continue
         others = ones_rows(blocks, lefts, 0)
         for n, k in enumerate(rights):
             term = lax.dot_general(
@@ -191,7 +193,7 @@
 
 
 def left_kernel(rows, points_left, left_sum, right_norm, *refs):
-    every, (sent, own, product, left_norm) = refs[: 2 * rows], refs[2 * rows :]
+    every, (sent, base, own, product, left_norm) = refs[: 2 * rows], refs[2 * rows :]
     blocks = {(i % rows, i // rows): x for i, x in enumerate(every)}
     last = (rows - 1, 1)
     size, width = left_sum.shape[1], left_sum.shape[2] // 2
@@ -203,68 +205,82 @@
             both = left_sum[index]
         else:
             both = jnp.dot(product[...], ones_rows(blocks, [(k, 0) for k in rights], 1), preferred_element_type=f32)
-        term = both[:, :width] - both[:, width:] * rows_of(every[index], 0, 0).astype(f32)
-        sent[index * size : (index + 1) * size, :] = term.astype(bf16)
+        wide = rows_of(every[index], 0, 0).astype(f32)
+        change = step_scale * (both[:, :width] - both[:, width:] * wide)
+        sent[index * size : (index + 1) * size, :] = change.astype(bf16)
+        base[index * size : (index + 1) * size, :] = wide - change
         if index == 0:
-            own[...] = points_left[...] - step_scale * term[: own.shape[0], :]
-
-
-def right_kernel(rows, points_right, right_sum, product, last, *refs):
-    near, (sent, own) = refs[:rows], refs[rows:]
+            own[...] = points_left[...] - change[: own.shape[0], :]
+
+
+def right_kernel(rows, summed, pieces, points_right, right_sum, *refs):
+    kept, refs = refs[: len(pieces)], refs[len(pieces) :]
+    every, (sent, norms, own) = refs[: 2 * rows], refs[2 * rows :]
+    blocks = {(i % rows, i // rows): x for i, x in enumerate(every)}
     size, width = right_sum.shape[1], right_sum.shape[2] // 2
-    others = with_ones(rows_of(last, 0, 0))
     for index in range(rows):
-        both = right_sum[index] + lax.dot_general(
-            product[:, index * size : (index + 1) * size], others, FIRST, preferred_element_type=f32
-        )
-        wide = rows_of(near[index], 1, 0).astype(f32)
+        terms = [right_sum[index]] if index in summed else []
+        for (lefts, rights), product in zip(pieces, kept):
+            if index in rights:
+                n = rights.index(index)
+                terms.append(
+                    lax.dot_general(
+                        product[:, n * size : (n + 1) * size],
+                        ones_rows(blocks, lefts, 0),
+                        FIRST,
+                        preferred_element_type=f32,
+                    )
+                )
+        both = sum(terms[1:], terms[0])
+        wide = rows_of(every[index], 1, 0).astype(f32)
         change = step_scale * (both[:, :width] - both[:, width:] * wide)
-        sent[index * size : (index + 1) * size, :] = (wide - change).astype(bf16)
+        new = (wide - change).astype(bf16)
+        sent[index * size : (index + 1) * size, :] = new
+        norms[:, index * size : (index + 1) * size] = norm_row(new)
         if index == 0:
             own[...] = points_right[...] - change[: own.shape[0], :]
 
 
-def own_weights_kernel(rows, *refs):
-    every, (left_weight, right_weight) = refs[: 2 * rows], refs[2 * rows :]
+def own_weights_kernel(rows, sets, *refs):
+    mine, every = refs[0], refs[1 : 1 + len(sets)]
+    left_weight, right_weight = refs[-2:]
     points = left_weight.shape[0]
     size = left_weight.shape[1] // (2 * rows)
     for side, out in ((0, left_weight), (1, right_weight)):
-        panel = every[0][side, 0, points:, :]
-        for index in range(2 * rows):
+        panel = mine[side, 0, points:, :]
+        for (k, half), ref in zip(sets, every):
+            index = half * rows + k
             out[:, index * size : (index + 1) * size] = lax.dot_general(
-                panel, rows_of(every[index], 1 - side, 1), LAST, preferred_element_type=f32
-            )
-
-
-def own_term(feat, weight, others):
+                panel, rows_of(ref, 1 - side, 1), LAST, preferred_element_type=f32
+            )
+
+
+def own_term(feat, weight, others, other_norm):
     crossed = lax.dot_general(feat, others, LAST, preferred_element_type=f32)
     wide = feat.astype(f32)
     norm = jnp.sum(wide * wide, axis=1, keepdims=True)
-    other_norm = norm_row(others)[0:1, :]
     kernel = jnp.exp2(exp2_scale * (2.0 * crossed - norm - other_norm))
     product = (weight * kernel).astype(bf16)
     total = jnp.sum(product.astype(f32), axis=1, keepdims=True)
     return jnp.dot(product, others, preferred_element_type=f32) - total * wide
 
 
-def last_right_kernel(rows, sent, came, own, weight, *refs):
-    every, (new, grad, others) = refs[: 2 * rows], refs[2 * rows :]
-    half = sent.shape[0] // 2
-    size = half // rows
-    for index in range(2 * rows):
-        mine = index * size
-        theirs = (mine + half) % (2 * half)
-        change = sent[mine : mine + size, :].astype(f32) + came[theirs : theirs + size, :].astype(f32)
-        feat = rows_of(every[index], 0, 0).astype(f32) - step_scale * change
-        others[mine : mine + size, :] = feat.astype(bf16)
+def last_right_kernel(base, came, own, weight, new, grad):
+    half = base.shape[0] // 2
+    others = [
+        (base[:half, :] - came[half:, :].astype(f32)).astype(bf16),
+        (base[half:, :] - came[:half, :].astype(f32)).astype(bf16),
+    ]
     value = own[...]
-    term = grad_scale * own_term(value.astype(bf16), weight[...], others[...])
+    norm = jnp.concatenate([norm_row(x)[0:1, :] for x in others], axis=1)
+    others = jnp.concatenate(others, axis=0)
+    term = grad_scale * own_term(value.astype(bf16), weight[...], others, norm)
     grad[...] = term
     new[...] = value - descent_rate * term
 
 
-def last_left_kernel(left_came, sent, came, own, weight, right_new, right_grad, *refs):
-    outs, (others, new, grad, sems) = refs[:4], refs[4:]
+def last_left_kernel(left_came, sent, sent_norm, came, own, weight, right_new, right_grad, *refs):
+    outs, (new, grad, sems) = refs[:4], refs[4:]
     copies = [
         pltpu.make_async_copy(x, out, sems.at[i])
         for i, (x, out) in enumerate(zip((right_new, right_grad, new, grad), (outs[1], outs[3], outs[0], outs[2])))
@@ -273,10 +289,10 @@
     copies[1].start()
     points = own.shape[0]
     half = sent.shape[0]
-    others[:half, :] = sent[...]
-    others[half:, :] = came[...]
-    value = own[...] - step_scale * left_came[half : half + points, :].astype(f32)
-    term = grad_scale * own_term(value.astype(bf16), weight[...], others[...])
+    others = jnp.concatenate([sent[...], came[...]], axis=0)
+    norm = jnp.concatenate([sent_norm[0:1, :], norm_row(came[...])[0:1, :]], axis=1)
+    value = own[...] - left_came[half : half + points, :].astype(f32)
+    term = grad_scale * own_term(value.astype(bf16), weight[...], others, norm)
     grad[...] = term
     new[...] = value - descent_rate * term
     copies[2].start()
@@ -337,9 +353,14 @@
         [pltpu.SemaphoreType.DMA((4,))],
         in_space=pl.ANY,
     )
-    across = jnp.concatenate([along_col(packed, k) for k in range(1, pairs)], axis=1)
+    line = [along_col(packed, k) for k in range(1, pairs)]
+    across = jnp.concatenate(line, axis=1)
     direct = [packed] + [along_row(packed, k) for k in range(1, rows)]
-    rest = [across] + [along_row(across, k) for k in range(1, rows)]
+    rest = [across] + [along_row(across, k) for k in range(1, rows - 1)]
+    own = jnp.concatenate([x for k, x in enumerate(line, 1) if k not in (1,)], axis=1)
+    own = jnp.split(along_row(own, rows - 1), pairs - 1 - len((1,)), axis=1)
+    parts = [along_col(direct[-1], k) if k in (1,) else own.pop(0) for k in range(1, pairs)]
+    rest.append(jnp.concatenate(parts, axis=1))
     blocks = {}
     for k in range(rows):
         near = jnp.concatenate([direct[k], rest[k]], axis=1)
@@ -355,66 +376,82 @@
     values = None
     seen_left, seen_right = set(), set()
 
-    def stage(rects, new_left, new_right):
+    def stage(rects, new_left, new_right, keep=False):
         nonlocal values
         sets = sorted({x for lefts, _ in rects for x in lefts} | {(k, 0) for _, rights in rects for k in rights})
         lefts = {x for part, _ in rects for x in part}
         rights = {k for _, part in rects for k in part}
-        plan = (rects, new_left, new_right, lefts - seen_left, rights - seen_right, values is None)
+        plan = (rects, new_left, new_right, lefts - seen_left, rights - seen_right, values is None, keep)
         seen_left.update(lefts)
-        seen_right.update(rights)
+        if not keep:
+            seen_right.update(rights)
+        places = [(len(a) * size, len(b) * size) for a, b in rects]
         inputs = [blocks[x] for x in sets] + list(values or ())
         values = call(
             functools.partial(stage_kernel, plan, sets),
             inputs,
-            state,
-            [pltpu.VMEM((max(len(a) for a, _ in rects) * size, max(len(b) for _, b in rects) * size), bf16)],
+            state + tuple(shape(x, bf16) for x in places if keep),
+            [] if keep else [pltpu.VMEM(tuple(max(x) for x in zip(*places)), bf16)],
             aliases={len(sets) + i: i for i in range(4)} if values else None,
             flops=sum(len(a) * len(b) for a, b in rects) * 12 * size * size * width,
         )
 
+    held = ()
+
+    def weights(sets):
+        return call(
+            functools.partial(own_weights_kernel, rows, sets),
+            [blocks[0, 0]] + [blocks[x] for x in sets] + list(held),
+            [shape((points, 2 * rows * size), f32)] * 2,
+            aliases={1 + len(sets) + i: i for i in range(2)} if held else None,
+        )
+
     waiting = []
     for k in range(rows):
+        if k == rows - 1:
+            held = weights([(i, half) for half in (0, 1) for i in range(k)])
         old = [(i, half) for half in (0, 1) for i in range(k) if (i, half) in seen_left]
         rects = ([(old, [k])] if old else []) + [([(k, 0)], list(range(k + 1)))]
-        stage(rects, [(k, 0)], [k])
+        stage(rects, [(k, 0)], [k], keep=k == rows - 1)
+        if k == rows - 1:
+            kept, values, pieces = values[4:], values[:4], rects
         waiting.append((k, 1))
         if k != 1 and k != rows - 1:
             stage([(waiting, list(range(k + 1)))], waiting, [])
             waiting = []
     if waiting[:-1]:
-        stage([(waiting[:-1], list(range(rows)))], waiting[:-1], [])
+        more = [(waiting[:-1], list(range(rows)))]
+        stage(more, waiting[:-1], [], keep=True)
+        kept, values, pieces = [*kept, *values[4:]], values[:4], pieces + more
     left_sum, right_sum, _, right_norm = values
     near = [blocks[k, 0] for k in range(rows)]
     every = near + [blocks[k, 1] for k in range(rows)]
-    left_sent, left_own, product = call(
+    left_sent, left_base, left_own, product = call(
         functools.partial(left_kernel, rows),
         [left_held, left_sum, right_norm] + every,
-        [shape((2 * rows * size, width), bf16), own_shape, shape((size, rows * size), bf16)],
+        [
+            shape((2 * rows * size, width), bf16),
+            shape((2 * rows * size, width), f32),
+            own_shape,
+            shape((size, rows * size), bf16),
+        ],
         [pltpu.VMEM((1, size, width), f32)],
     )
     left_came = partner(left_sent)
-    right_sent, right_own = call(
-        functools.partial(right_kernel, rows),
-        [right_held, right_sum, product, blocks[rows - 1, 1]] + near,
-        [shape((rows * size, width), bf16), own_shape],
+    pieces = pieces + [([(rows - 1, 1)], list(range(rows)))]
+    right_sent, right_row_norm, right_own = call(
+        functools.partial(right_kernel, rows, seen_right, pieces),
+        [right_held, right_sum, *kept, product] + every,
+        [shape((rows * size, width), bf16), shape((8, rows * size), f32), own_shape],
     )
     right_came = partner(right_sent)
-    left_weight, right_weight = call(
-        functools.partial(own_weights_kernel, rows), every, [shape((points, 2 * rows * size), f32)] * 2
-    )
-    scratch = [pltpu.VMEM((2 * rows * size, width), bf16)]
-    right_new, right_grad = call(
-        functools.partial(last_right_kernel, rows),
-        [left_sent, left_came, right_own, right_weight] + every,
-        [own_shape] * 2,
-        scratch,
-    )
+    left_weight, right_weight = weights([(rows - 1, 0), (rows - 1, 1)])
+    right_new, right_grad = call(last_right_kernel, [left_base, left_came, right_own, right_weight], [own_shape] * 2)
     return call(
         last_left_kernel,
-        [left_came, right_sent, right_came, left_own, left_weight, right_new, right_grad],
+        [left_came, right_sent, right_row_norm, right_came, left_own, left_weight, right_new, right_grad],
         [own_shape] * 4,
-        scratch + [pltpu.VMEM((points, width), f32)] * 2 + [pltpu.SemaphoreType.DMA((4,))],
+        [pltpu.VMEM((points, width), f32)] * 2 + [pltpu.SemaphoreType.DMA((4,))],
         out_space=pltpu.HBM,
     )
 

time: 35.7 us -> 35.2 us (0.986)
  waiting for transfers between devices: 8.63 us -> 8.03 us
  Pallas kernels: 10.3 us -> 10.8 us
  starting transfers between devices: 15.6 us -> 15.1 us
    ppermute x6, waiting for transfers between devices: 8.12 us -> 5.55 us  [along_row(): return lax.ppermute(x, 'row', [(i, target(i)) for i in range(rows)])]
    ppermute x3 -> x4, waiting for transfers between devices: 0.01 us -> 2.32 us  [along_col(): lax.ppermute(x, 'col', [(i, (i + 2 * k) % cols) for i in range(cols)])]
    ppermute x6, starting transfers between devices: 1.41 us -> 0.87 us  [partner(): return lax.ppermute(x, 'col', [(i, i ^ 1) for i in range(cols)])]
    pallas_call x12 -> x13, Pallas kernels: 10.3 us -> 10.8 us  [call(): pl.pallas_call(kernel, out_shape=tuple(outputs), in_specs=[pl.BlockSpec(m...]
    ppermute x3 -> x4, starting transfers between devices: 7.04 us -> 7.19 us  [along_col(): lax.ppermute(x, 'col', [(i, (i + 2 * k) % cols) for i in range(cols)])]
  transfers between devices with their start and end apart: 15 -> 16, of which waited for: 3 -> 5; matrix products, arithmetic and copies ran while one was open for 1% -> 1% of each run, Pallas kernels for 21% -> 23%
where the time goes in v2:
time: 35.2 us; the launch traced here: 35 us
  starting transfers between devices  15.1 us (43%)
  Pallas kernels  10.8 us (31%)
  waiting for transfers between devices  8.03 us (23%)
  between operations  0.86 us (2%)
    pallas_call x13, Pallas kernels, call(): pl.pallas_call(kernel, out_shape=tuple(outputs), in_specs=[pl.BlockSpec(m...  10.8 us
    ppermute x4, starting transfers between devices, along_col(): lax.ppermute(x, 'col', [(i, (i + 2 * k) % cols) for i in range(cols)])  7.19 us
    ppermute x6, starting transfers between devices, along_row(): return lax.ppermute(x, 'row', [(i, target(i)) for i in range(rows)])  7.07 us
    ppermute x6, waiting for transfers between devices, along_row(): return lax.ppermute(x, 'row', [(i, target(i)) for i in range(rows)])  5.55 us
    ppermute x4, waiting for transfers between devices, along_col(): lax.ppermute(x, 'col', [(i, (i + 2 * k) % cols) for i in range(cols)])  2.32 us
    ppermute x6, starting transfers between devices, partner(): return lax.ppermute(x, 'col', [(i, i ^ 1) for i in range(cols)])  0.87 us
  transfers between devices with their start and end apart: 16, of which 5 were waited for; matrix products, arithmetic and copies ran while one was open for 1% of the time, Pallas kernels for 23%

profile of v2, /device:TPU:0, one launch (start us, length us, event | category | flops | bytes accessed | tf_op | source)
XLA Modules:
  0.0 35.0 jit_solution(6366794062992682026)
XLA Ops:
  0.6 0.8 %shard_map.75 = (bf16[2,128,128]{2,1,0:T(8,128)(2,1)S(1)}, f32[64,128]{1,0:T(8,128)S(1)}, f32[64,128]{1,0:T(8,128)S(1)}) custom-call(f32[64,128]{1,0:T(8,128)} %left.1, f32[64,128]{1,0:T(8,128)} %right.1, bf16[64,128]{1,0:T(8,128)(2,1)} %left_panel.1, bf16[64,128]{1,0:T(8,128)(2,1)} %right_panel.1), custom_call_target="tpu_custom_call" | custom-call | bytes 28672 | tf_op jit(solution)/shard_map/pallas_call | solution.py:318
  1.5 3.1 %collective-permute-start = (bf16[2,128,128]{2,1,0:T(8,128)(2,1)S(1)}, bf16[2,128,128]{2,1,0:T(8,128)(2,1)S(1)}, u32[]{:S(2)}, u32[]{:S(2)}) collective-permute-start(bf16[2,128,128]{2,1,0:T(8,128)(2,1)S(1)} %get-tuple-element.46), channel_id=1, source_target_pairs={{0,2},{1,3},{2,4},{3,5},{4,6},{5,7},{6,0},{7,1},{8,10},{9,11},{10,... | collective-permute-start | bytes 196616 | tf_op jit(solution)/shard_map/ppermute | solution.py:337
  4.6 2.6 %collective-permute-start.1 = (bf16[2,128,128]{2,1,0:T(8,128)(2,1)S(1)}, bf16[2,128,128]{2,1,0:T(8,128)(2,1)S(1)}, u32[]{:S(2)}, u32[]{:S(2)}) collective-permute-start(bf16[2,128,128]{2,1,0:T(8,128)(2,1)S(1)} %get-tuple-element.46), channel_id=1, source_target_pairs={{0,4},{1,5},{2,6},{3,7},{4,0},{5,1},{6,2},{7,3},{8,12},{9,13},{10,... | collective-permute-start | bytes 196616 | tf_op jit(solution)/shard_map/ppermute | solution.py:337
  7.2 1.3 %collective-permute-start.2 = (bf16[2,128,128]{2,1,0:T(8,128)(2,1)S(1)}, bf16[2,128,128]{2,1,0:T(8,128)(2,1)S(1)}, u32[]{:S(2)}, u32[]{:S(2)}) collective-permute-start(bf16[2,128,128]{2,1,0:T(8,128)(2,1)S(1)} %get-tuple-element.46), channel_id=1, source_target_pairs={{0,6},{1,7},{2,0},{3,1},{4,2},{5,3},{6,4},{7,5},{8,14},{9,15},{10,... | collective-permute-start | bytes 196616 | tf_op jit(solution)/shard_map/ppermute | solution.py:337
  8.5 1.5 %collective-permute-start.4 = (bf16[2,128,128]{2,1,0:T(8,128)(2,1)S(1)}, bf16[2,128,128]{2,1,0:T(8,128)(2,1)S(1)}, u32[]{:S(2)}, u32[]{:S(2)}) collective-permute-start(bf16[2,128,128]{2,1,0:T(8,128)(2,1)S(1)} %get-tuple-element.46), channel_id=1, source_target_pairs={{0,8},{8,0},{16,24},{24,16},{1,9},{9,1},{17,25},{25,17},{2,10},{10... | collective-permute-start | bytes 196616 | tf_op jit(solution)/shard_map/ppermute | solution.py:343
  10.0 1.5 %collective-permute-start.7 = (bf16[2,128,128]{2,1,0:T(8,128)(2,1)S(1)}, bf16[2,128,128]{2,1,0:T(8,128)(2,1)S(1)}, u32[]{:S(2)}, u32[]{:S(2)}) collective-permute-start(bf16[2,128,128]{2,1,0:T(8,128)(2,1)S(1)} %get-tuple-element.46), channel_id=1, source_target_pairs={{0,16},{8,24},{16,0},{24,8},{1,17},{9,25},{17,1},{25,9},{2,18},{10... | collective-permute-start | bytes 196616 | tf_op jit(solution)/shard_map/ppermute | solution.py:343
  11.5 0.5 %collective-permute-start.10 = (bf16[2,128,128]{2,1,0:T(8,128)(2,1)S(1)}, bf16[2,128,128]{2,1,0:T(8,128)(2,1)S(1)}, u32[]{:S(2)}, u32[]{:S(2)}) collective-permute-start(bf16[2,128,128]{2,1,0:T(8,128)(2,1)S(1)} %get-tuple-element.46), channel_id=1, source_target_pairs={{0,24},{8,16},{16,8},{24,0},{1,25},{9,17},{17,9},{25,1},{2,26},{10... | collective-permute-start | bytes 196616 | tf_op jit(solution)/shard_map/ppermute | solution.py:343
  12.2 1.6 %collective-permute-start.5 = (bf16[2,384,128]{2,1,0:T(8,128)(2,1)S(1)}, bf16[2,384,128]{2,1,0:T(8,128)(2,1)S(1)}, u32[]{:S(2)}, u32[]{:S(2)}) collective-permute-start(bf16[2,384,128]{2,1,0:T(8,128)(2,1)S(1)} %get-tuple-element.86), channel_id=1, source_target_pairs={{0,8},{8,0},{16,24},{24,16},{1,9},{9,1},{17,25},{25,17},{2,10},{10... | collective-permute-start | bytes 589832 | tf_op jit(solution)/shard_map/ppermute | solution.py:343
  13.7 1.5 %collective-permute-start.8 = (bf16[2,384,128]{2,1,0:T(8,128)(2,1)S(1)}, bf16[2,384,128]{2,1,0:T(8,128)(2,1)S(1)}, u32[]{:S(2)}, u32[]{:S(2)}) collective-permute-start(bf16[2,384,128]{2,1,0:T(8,128)(2,1)S(1)} %get-tuple-element.86), channel_id=1, source_target_pairs={{0,16},{8,24},{16,0},{24,8},{1,17},{9,25},{17,1},{25,9},{2,18},{10... | collective-permute-start | bytes 589832 | tf_op jit(solution)/shard_map/ppermute | solution.py:343
  15.4 2.1 %collective-permute-done.10 = bf16[2,128,128]{2,1,0:T(8,128)(2,1)S(1)} collective-permute-done((bf16[2,128,128]{2,1,0:T(8,128)(2,1)S(1)}, bf16[2,128,128]{2,1,0:T(8,128)(2,1)S(1)}, u32[]{:S(2)}, u32[]{:S(2)}) %collective-permute-start.10) | collective-permute-done | bytes 65568 | tf_op jit(solution)/shard_map/ppermute | solution.py:343
  18.1 1.6 %collective-permute-done.5 = bf16[2,384,128]{2,1,0:T(8,128)(2,1)S(1)} collective-permute-done((bf16[2,384,128]{2,1,0:T(8,128)(2,1)S(1)}, bf16[2,384,128]{2,1,0:T(8,128)(2,1)S(1)}, u32[]{:S(2)}, u32[]{:S(2)}) %collective-permute-start.5) | collective-permute-done | bytes 196640 | tf_op jit(solution)/shard_map/ppermute | solution.py:343
  19.8 1.8 %collective-permute-done.8 = bf16[2,384,128]{2,1,0:T(8,128)(2,1)S(1)} collective-permute-done((bf16[2,384,128]{2,1,0:T(8,128)(2,1)S(1)}, bf16[2,384,128]{2,1,0:T(8,128)(2,1)S(1)}, u32[]{:S(2)}, u32[]{:S(2)}) %collective-permute-start.8) | collective-permute-done | bytes 196640 | tf_op jit(solution)/shard_map/ppermute | solution.py:343
  21.7 2.3 %collective-permute-done.11 = bf16[2,128,128]{2,1,0:T(8,128)(2,1)S(1)} collective-permute-done((bf16[2,128,128]{2,1,0:T(8,128)(2,1)S(1)}, bf16[2,128,128]{2,1,0:T(8,128)(2,1)S(1)}, u32[]{:S(2)}, u32[]{:S(2)}) %collective-permute-start.11) | collective-permute-done | bytes 65568 | tf_op jit(solution)/shard_map/ppermute | solution.py:337
  24.2 0.5 %shard_map.76 = (f32[8,256,256]{2,1,0:T(8,128)S(1)}, f32[4,256,256]{2,1,0:T(8,128)S(1)}, f32[8,256,128]{2,1,0:T(8,128)S(1)}, f32[4,8,256]{2,1,0:T(8,128)S(1)}) custom-call(bf16[2,4,128,128]{3,2,1,0:T(8,128)(2,1)S(1)} %bitcast.8), custom_call_target="tpu_custom_call" | custom-call | flops 100663296 | bytes 561152 | tf_op jit(solution)/shard_map/pallas_call | solution.py:318
  24.7 0.5 %shard_map.77 = (f32[8,256,256]{2,1,0:T(8,128)S(1)}, f32[4,256,256]{2,1,0:T(8,128)S(1)}, f32[8,256,128]{2,1,0:T(8,128)S(1)}, f32[4,8,256]{2,1,0:T(8,128)S(1)}) custom-call(bf16[2,4,128,128]{3,2,1,0:T(8,128)(2,1)S(1)} %bitcast.9, bf16[2,4,128,128]{3,2,1,0:T(8,128)(2,1)S(1)} %bitcast.26, ...), custom_call_target="tpu_custom_call", output_to_operand_aliasing={{0}: (2, {}), {1}: (3, {}), {2}: (4, {}), {3}: (5, {})} | custom-call | flops 100663296 | bytes 1122304 | tf_op jit(solution)/shard_map/pallas_call | solution.py:318
  25.2 0.9 %shard_map.78 = (f32[8,256,256]{2,1,0:T(8,128)S(1)}, f32[4,256,256]{2,1,0:T(8,128)S(1)}, f32[8,256,128]{2,1,0:T(8,128)S(1)}, f32[4,8,256]{2,1,0:T(8,128)S(1)}) custom-call(bf16[2,4,128,128]{3,2,1,0:T(8,128)(2,1)S(1)} %bitcast.10, bf16[2,4,128,128]{3,2,1,0:T(8,128)(2,1)S(1)} %bitcast.27, ...), custom_call_target="tpu_custom_call", output_to_operand_aliasing={{0}: (3, {}), {1}: (4, {}), {2}: (5, {}), {3}: (6, {})} | custom-call | flops 402653184 | bytes 1155072 | tf_op jit(solution)/shard_map/pallas_call | solution.py:318
  26.1 1.1 %shard_map.79 = (f32[8,256,256]{2,1,0:T(8,128)S(1)}, f32[4,256,256]{2,1,0:T(8,128)S(1)}, f32[8,256,128]{2,1,0:T(8,128)S(1)}, f32[4,8,256]{2,1,0:T(8,128)S(1)}) custom-call(bf16[2,4,128,128]{3,2,1,0:T(8,128)(2,1)S(1)} %bitcast.11, bf16[2,4,128,128]{3,2,1,0:T(8,128)(2,1)S(1)} %bitcast.28, ...), custom_call_target="tpu_custom_call", output_to_operand_aliasing={{0}: (4, {}), {1}: (5, {}), {2}: (6, {}), {3}: (7, {})} | custom-call | flops 603979776 | bytes 1187840 | tf_op jit(solution)/shard_map/pallas_call | solution.py:318
  27.2 1.0 %shard_map.80 = (f32[8,256,256]{2,1,0:T(8,128)S(1)}, f32[4,256,256]{2,1,0:T(8,128)S(1)}, f32[8,256,128]{2,1,0:T(8,128)S(1)}, f32[4,8,256]{2,1,0:T(8,128)S(1)}) custom-call(bf16[2,4,128,128]{3,2,1,0:T(8,128)(2,1)S(1)} %bitcast.12, bf16[2,4,128,128]{3,2,1,0:T(8,128)(2,1)S(1)} %bitcast.21, ...), custom_call_target="tpu_custom_call", output_to_operand_aliasing={{0}: (5, {}), {1}: (6, {}), {2}: (7, {}), {3}: (8, {})} | custom-call | flops 603979776 | bytes 1220608 | tf_op jit(solution)/shard_map/pallas_call | solution.py:318
  28.3 1.3 %shard_map.81 = (f32[8,256,256]{2,1,0:T(8,128)S(1)}, f32[4,256,256]{2,1,0:T(8,128)S(1)}, f32[8,256,128]{2,1,0:T(8,128)S(1)}, f32[4,8,256]{2,1,0:T(8,128)S(1)}, b...) custom-call(bf16[2,4,128,128]{3,2,1,0:T(8,128)(2,1)S(1)} %bitcast.13, ...), custom_call_target="tpu_custom_call", output_to_operand_aliasing={{0}: (7, {}), {1}: (8, {}), {2}: (9, {}), {3}: (10, {})} | custom-call | flops 1006632960 | bytes 1449984 | tf_op jit(solution)/shard_map/pallas_call | solution.py:318
  29.6 0.8 %shard_map.82 = (bf16[2048,128]{1,0:T(8,128)(2,1)S(1)}, f32[2048,128]{1,0:T(8,128)S(1)}, f32[64,128]{1,0:T(8,128)S(1)}, bf16[256,1024]{1,0:T(8,128)(2,1)S(1)}) custom-call(f32[64,128]{1,0:T(8,128)S(1)} %get-tuple-element.45.points_left, f32[8,256,256]{2,1,0:T(8,128)S(1)} %get-tuple-element.67.left_sum, f32[4,8,256]{2,1,0:T(8,128)S(1)} %get-tuple-element.68.right_norm, ...), custom_call_target="tpu_custom_call" | custom-call | bytes 798720 | tf_op jit(solution)/shard_map/pallas_call | solution.py:318
  30.4 0.6 %collective-permute-start.14 = (bf16[2048,128]{1,0:T(8,128)(2,1)S(1)}, bf16[2048,128]{1,0:T(8,128)(2,1)S(1)}, u32[]{:S(2)}, u32[]{:S(2)}) collective-permute-start(bf16[2048,128]{1,0:T(8,128)(2,1)S(1)} %get-tuple-element.69), channel_id=1, source_target_pairs={{0,1},{1,0},{2,3},{3,2},{4,5},{5,4},{6,7},{7,6},{8,9},{9,8},{10,11... | collective-permute-start | bytes 1572872 | tf_op jit(solution)/shard_map/ppermute | solution.py:346
  31.0 1.2 %shard_map.83 = (bf16[1024,128]{1,0:T(8,128)(2,1)S(1)}, f32[8,1024]{1,0:T(8,128)S(1)}, f32[64,128]{1,0:T(8,128)S(1)}) custom-call(f32[64,128]{1,0:T(8,128)S(1)} %get-tuple-element.70.points_right, f32[4,256,256]{2,1,0:T(8,128)S(1)} %get-tuple-element.71.right_sum, bf16[1536,256]{1,0:T(8,128)(2,1)S(1)} %get-tuple-element.72.refs_0_, ...), custom_call_target="tpu_custom_call" | custom-call | bytes 667648 | tf_op jit(solution)/shard_map/pallas_call | solution.py:318
  32.8 0.8 %shard_map.86 = (f32[64,128]{1,0:T(8,128)S(1)}, f32[64,128]{1,0:T(8,128)S(1)}) custom-call(f32[2048,128]{1,0:T(8,128)S(1)} %get-tuple-element.81.base, bf16[2048,128]{1,0:T(8,128)(2,1)S(1)} %collective-permute-done.14.came.left_came, f32[64,128]{1,0:T(8,128)S(1)} %get-tuple-element.82.own, f32[64,2048]{1,0:T(8,128)S(1)} %get-tuple-element.83.weight), custom_call_target="tpu_custom_call" | custom-call | bytes 274432 | tf_op jit(solution)/shard_map/pallas_call | solution.py:318
  33.7 1.3 %shard_map.87 = (f32[64,128]{1,0:T(8,128)}, f32[64,128]{1,0:T(8,128)}, f32[64,128]{1,0:T(8,128)}, f32[64,128]{1,0:T(8,128)}) custom-call(bf16[2048,128]{1,0:T(8,128)(2,1)S(1)} %collective-permute-done.14.came.left_came, bf16[1024,128]{1,0:T(8,128)(2,1)S(1)} %get-tuple-element.75.sent, f32[8,1024]{1,0:T(8,128)S(1)} %get-tuple-element.76.sent_norm, ...), custom_call_target="tpu_custom_call" | custom-call | bytes 229376 | tf_op jit(solution)/shard_map/pallas_call | solution.py:318
  (33 shorter events, 1.9 us)
Async XLA Ops:
  1.5 10.1 %collective-permute-start = (bf16[2,128,128]{2,1,0:T(8,128)(2,1)S(1)}, bf16[2,128,128]{2,1,0:T(8,128)(2,1)S(1)}, u32[]{:S(2)}, u32[]{:S(2)}) collective-permute-start(bf16[2,128,128]{2,1,0:T(8,128)(2,1)S(1)} %get-tuple-element.46), channel_id=1, source_target_pairs={{0,2},{1,3},{2,4},{3,5},{4,6},{5,7},{6,0},{7,1},{8,10},{9,11},{10,... | collective-permute-start | bytes 196616 | tf_op jit(solution)/shard_map/ppermute | solution.py:337
  4.6 7.5 %collective-permute-start.1 = (bf16[2,128,128]{2,1,0:T(8,128)(2,1)S(1)}, bf16[2,128,128]{2,1,0:T(8,128)(2,1)S(1)}, u32[]{:S(2)}, u32[]{:S(2)}) collective-permute-start(bf16[2,128,128]{2,1,0:T(8,128)(2,1)S(1)} %get-tuple-element.46), channel_id=1, source_target_pairs={{0,4},{1,5},{2,6},{3,7},{4,0},{5,1},{6,2},{7,3},{8,12},{9,13},{10,... | collective-permute-start | bytes 196616 | tf_op jit(solution)/shard_map/ppermute | solution.py:337
  7.2 5.0 %collective-permute-start.2 = (bf16[2,128,128]{2,1,0:T(8,128)(2,1)S(1)}, bf16[2,128,128]{2,1,0:T(8,128)(2,1)S(1)}, u32[]{:S(2)}, u32[]{:S(2)}) collective-permute-start(bf16[2,128,128]{2,1,0:T(8,128)(2,1)S(1)} %get-tuple-element.46), channel_id=1, source_target_pairs={{0,6},{1,7},{2,0},{3,1},{4,2},{5,3},{6,4},{7,5},{8,14},{9,15},{10,... | collective-permute-start | bytes 196616 | tf_op jit(solution)/shard_map/ppermute | solution.py:337
  8.5 6.8 %collective-permute-start.4 = (bf16[2,128,128]{2,1,0:T(8,128)(2,1)S(1)}, bf16[2,128,128]{2,1,0:T(8,128)(2,1)S(1)}, u32[]{:S(2)}, u32[]{:S(2)}) collective-permute-start(bf16[2,128,128]{2,1,0:T(8,128)(2,1)S(1)} %get-tuple-element.46), channel_id=1, source_target_pairs={{0,8},{8,0},{16,24},{24,16},{1,9},{9,1},{17,25},{25,17},{2,10},{10... | collective-permute-start | bytes 196616 | tf_op jit(solution)/shard_map/ppermute | solution.py:343
  10.0 8.0 %collective-permute-start.7 = (bf16[2,128,128]{2,1,0:T(8,128)(2,1)S(1)}, bf16[2,128,128]{2,1,0:T(8,128)(2,1)S(1)}, u32[]{:S(2)}, u32[]{:S(2)}) collective-permute-start(bf16[2,128,128]{2,1,0:T(8,128)(2,1)S(1)} %get-tuple-element.46), channel_id=1, source_target_pairs={{0,16},{8,24},{16,0},{24,8},{1,17},{9,25},{17,1},{25,9},{2,18},{10... | collective-permute-start | bytes 196616 | tf_op jit(solution)/shard_map/ppermute | solution.py:343
  11.5 6.0 %collective-permute-start.10 = (bf16[2,128,128]{2,1,0:T(8,128)(2,1)S(1)}, bf16[2,128,128]{2,1,0:T(8,128)(2,1)S(1)}, u32[]{:S(2)}, u32[]{:S(2)}) collective-permute-start(bf16[2,128,128]{2,1,0:T(8,128)(2,1)S(1)} %get-tuple-element.46), channel_id=1, source_target_pairs={{0,24},{8,16},{16,8},{24,0},{1,25},{9,17},{17,9},{25,1},{2,26},{10... | collective-permute-start | bytes 196616 | tf_op jit(solution)/shard_map/ppermute | solution.py:343
  12.2 7.5 %collective-permute-start.5 = (bf16[2,384,128]{2,1,0:T(8,128)(2,1)S(1)}, bf16[2,384,128]{2,1,0:T(8,128)(2,1)S(1)}, u32[]{:S(2)}, u32[]{:S(2)}) collective-permute-start(bf16[2,384,128]{2,1,0:T(8,128)(2,1)S(1)} %get-tuple-element.86), channel_id=1, source_target_pairs={{0,8},{8,0},{16,24},{24,16},{1,9},{9,1},{17,25},{25,17},{2,10},{10... | collective-permute-start | bytes 589832 | tf_op jit(solution)/shard_map/ppermute | solution.py:343
  13.7 7.9 %collective-permute-start.8 = (bf16[2,384,128]{2,1,0:T(8,128)(2,1)S(1)}, bf16[2,384,128]{2,1,0:T(8,128)(2,1)S(1)}, u32[]{:S(2)}, u32[]{:S(2)}) collective-permute-start(bf16[2,384,128]{2,1,0:T(8,128)(2,1)S(1)} %get-tuple-element.86), channel_id=1, source_target_pairs={{0,16},{8,24},{16,0},{24,8},{1,17},{9,25},{17,1},{25,9},{2,18},{10... | collective-permute-start | bytes 589832 | tf_op jit(solution)/shard_map/ppermute | solution.py:343
  15.3 9.4 %collective-permute-start.3 = (bf16[2,512,128]{2,1,0:T(8,128)(2,1)S(1)}, bf16[2,512,128]{2,1,0:T(8,128)(2,1)S(1)}, u32[]{:S(2)}, u32[]{:S(2)}) collective-permute-start(bf16[2,512,128]{2,1,0:T(8,128)(2,1)S(1)} %get-tuple-element.87), channel_id=1, source_target_pairs={{0,1},{1,0},{2,3},{3,2},{4,5},{5,4},{6,7},{7,6},{8,9},{9,8},{10,11... | collective-permute-start | bytes 786440 | tf_op jit(solution)/shard_map/ppermute | solution.py:346
  17.5 6.6 %collective-permute-start.12 = (bf16[2,256,128]{2,1,0:T(8,128)(2,1)S(1)}, bf16[2,256,128]{2,1,0:T(8,128)(2,1)S(1)}, u32[]{:S(2)}, u32[]{:S(2)}) collective-permute-start(bf16[2,256,128]{2,1,0:T(8,128)(2,1)S(1)} %pad_maximum_fusion), channel_id=1, source_target_pairs={{0,24},{8,16},{16,8},{24,0},{1,25},{9,17},{17,9},{25,1},{2,26},{10... | collective-permute-start | bytes 393224 | tf_op jit(solution)/shard_map/ppermute | solution.py:343
  17.9 6.1 %collective-permute-start.11 = (bf16[2,128,128]{2,1,0:T(8,128)(2,1)S(1)}, bf16[2,128,128]{2,1,0:T(8,128)(2,1)S(1)}, u32[]{:S(2)}, u32[]{:S(2)}) collective-permute-start(bf16[2,128,128]{2,1,0:T(8,128)(2,1)S(1)} %collective-permute-done.10), channel_id=1, source_target_pairs={{0,2},{1,3},{2,4},{3,5},{4,6},{5,7},{6,0},{7,1},{8,10},{9,11},{10,... | collective-permute-start | bytes 196616 | tf_op jit(solution)/shard_map/ppermute | solution.py:337
  19.8 7.5 %collective-permute-start.6 = (bf16[2,512,128]{2,1,0:T(8,128)(2,1)S(1)}, bf16[2,512,128]{2,1,0:T(8,128)(2,1)S(1)}, u32[]{:S(2)}, u32[]{:S(2)}) collective-permute-start(bf16[2,512,128]{2,1,0:T(8,128)(2,1)S(1)} %constant_dynamic-update-slice_fusion.7), channel_id=1, source_target_pairs={{0,1},{1,0},{2,3},{3,2},{4,5},{5,4},{6,7},{7,6},{8,9},{9,8},{10,11... | collective-permute-start | bytes 786440 | tf_op jit(solution)/shard_map/ppermute | solution.py:346
  21.7 5.6 %collective-permute-start.9 = (bf16[2,512,128]{2,1,0:T(8,128)(2,1)S(1)}, bf16[2,512,128]{2,1,0:T(8,128)(2,1)S(1)}, u32[]{:S(2)}, u32[]{:S(2)}) collective-permute-start(bf16[2,512,128]{2,1,0:T(8,128)(2,1)S(1)} %constant_dynamic-update-slice_fusion.9), channel_id=1, source_target_pairs={{0,1},{1,0},{2,3},{3,2},{4,5},{5,4},{6,7},{7,6},{8,9},{9,8},{10,11... | collective-permute-start | bytes 786440 | tf_op jit(solution)/shard_map/ppermute | solution.py:346
  24.1 5.5 %collective-permute-start.13 = (bf16[2,512,128]{2,1,0:T(8,128)(2,1)S(1)}, bf16[2,512,128]{2,1,0:T(8,128)(2,1)S(1)}, u32[]{:S(2)}, u32[]{:S(2)}) collective-permute-start(bf16[2,512,128]{2,1,0:T(8,128)(2,1)S(1)} %constant_dynamic-update-slice_fusion.11), channel_id=1, source_target_pairs={{0,1},{1,0},{2,3},{3,2},{4,5},{5,4},{6,7},{7,6},{8,9},{9,8},{10,11... | collective-permute-start | bytes 786440 | tf_op jit(solution)/shard_map/ppermute | solution.py:346
  30.4 2.4 %collective-permute-start.14 = (bf16[2048,128]{1,0:T(8,128)(2,1)S(1)}, bf16[2048,128]{1,0:T(8,128)(2,1)S(1)}, u32[]{:S(2)}, u32[]{:S(2)}) collective-permute-start(bf16[2048,128]{1,0:T(8,128)(2,1)S(1)} %get-tuple-element.69), channel_id=1, source_target_pairs={{0,1},{1,0},{2,3},{3,2},{4,5},{5,4},{6,7},{7,6},{8,9},{9,8},{10,11... | collective-permute-start | bytes 1572872 | tf_op jit(solution)/shard_map/ppermute | solution.py:346
  32.2 1.5 %collective-permute-start.15 = (bf16[1024,128]{1,0:T(8,128)(2,1)S(1)}, bf16[1024,128]{1,0:T(8,128)(2,1)S(1)}, u32[]{:S(2)}, u32[]{:S(2)}) collective-permute-start(bf16[1024,128]{1,0:T(8,128)(2,1)S(1)} %get-tuple-element.75.sent), channel_id=1, source_target_pairs={{0,1},{1,0},{2,3},{3,2},{4,5},{5,4},{6,7},{7,6},{8,9},{9,8},{10,11... | collective-permute-start | bytes 786440 | tf_op jit(solution)/shard_map/ppermute | solution.py:346

commit v3 on v2

--- a/solution.py
+++ b/solution.py
@@ -265,21 +265,25 @@
     return jnp.dot(product, others, preferred_element_type=f32) - total * wide
 
 
-def last_right_kernel(base, came, own, weight, new, grad):
-    half = base.shape[0] // 2
+def last_right_kernel(base, came, sent, sent_norm, own_right, own_left, right_weight, left_weight, *outs):
+    new, grad, left_value, left_term = outs
+    half, points = sent.shape[0], own_left.shape[0]
+    left = own_left[...] - came[half : half + points, :].astype(f32)
+    left_value[...] = left
+    left_term[...] = own_term(left.astype(bf16), left_weight[:, :half], sent[...], sent_norm[0:1, :])
     others = [
         (base[:half, :] - came[half:, :].astype(f32)).astype(bf16),
         (base[half:, :] - came[:half, :].astype(f32)).astype(bf16),
     ]
-    value = own[...]
     norm = jnp.concatenate([norm_row(x)[0:1, :] for x in others], axis=1)
     others = jnp.concatenate(others, axis=0)
-    term = grad_scale * own_term(value.astype(bf16), weight[...], others, norm)
+    value = own_right[...]
+    term = grad_scale * own_term(value.astype(bf16), right_weight[...], others, norm)
     grad[...] = term
     new[...] = value - descent_rate * term
 
 
-def last_left_kernel(left_came, sent, sent_norm, came, own, weight, right_new, right_grad, *refs):
+def last_left_kernel(came, left_value, left_term, weight, right_new, right_grad, *refs):
     outs, (new, grad, sems) = refs[:4], refs[4:]
     copies = [
         pltpu.make_async_copy(x, out, sems.at[i])
@@ -287,12 +291,11 @@
     ]
     copies[0].start()
     copies[1].start()
-    points = own.shape[0]
-    half = sent.shape[0]
-    others = jnp.concatenate([sent[...], came[...]], axis=0)
-    norm = jnp.concatenate([sent_norm[0:1, :], norm_row(came[...])[0:1, :]], axis=1)
-    value = own[...] - left_came[half : half + points, :].astype(f32)
-    term = grad_scale * own_term(value.astype(bf16), weight[...], others, norm)
+    half = came.shape[0]
+    value = left_value[...]
+    others = came[...]
+    term = left_term[...] + own_term(value.astype(bf16), weight[:, half:], others, norm_row(others)[0:1, :])
+    term = grad_scale * term
     grad[...] = term
     new[...] = value - descent_rate * term
     copies[2].start()
@@ -446,10 +449,14 @@
     )
     right_came = partner(right_sent)
     left_weight, right_weight = weights([(rows - 1, 0), (rows - 1, 1)])
-    right_new, right_grad = call(last_right_kernel, [left_base, left_came, right_own, right_weight], [own_shape] * 2)
+    right_new, right_grad, left_value, left_term = call(
+        last_right_kernel,
+        [left_base, left_came, right_sent, right_row_norm, right_own, left_own, right_weight, left_weight],
+        [own_shape] * 4,
+    )
     return call(
         last_left_kernel,
-        [left_came, right_sent, right_row_norm, right_came, left_own, left_weight, right_new, right_grad],
+        [right_came, left_value, left_term, left_weight, right_new, right_grad],
         [own_shape] * 4,
         [pltpu.VMEM((points, width), f32)] * 2 + [pltpu.SemaphoreType.DMA((4,))],
         out_space=pltpu.HBM,

time: 35.2 us -> 35.2 us (level)
  transfers between devices with their start and end apart: 16 -> 16, of which waited for: 5 -> 4; matrix products, arithmetic and copies ran while one was open for 1% -> 1% of each run, Pallas kernels for 23% -> 23%
where the time goes in v3:
time: 35.2 us; the launch traced here: 35 us
  starting transfers between devices  15.1 us (43%)
  Pallas kernels  10.9 us (31%)
  waiting for transfers between devices  7.89 us (22%)
  between operations  0.87 us (2%)
    pallas_call x13, Pallas kernels, call(): pl.pallas_call(kernel, out_shape=tuple(outputs), in_specs=[pl.BlockSpec(m...  10.9 us
    ppermute x4, starting transfers between devices, along_col(): lax.ppermute(x, 'col', [(i, (i + 2 * k) % cols) for i in range(cols)])  7.19 us
    ppermute x6, starting transfers between devices, along_row(): return lax.ppermute(x, 'row', [(i, target(i)) for i in range(rows)])  7.07 us
    ppermute x6, waiting for transfers between devices, along_row(): return lax.ppermute(x, 'row', [(i, target(i)) for i in range(rows)])  5.55 us
    ppermute x4, waiting for transfers between devices, along_col(): lax.ppermute(x, 'col', [(i, (i + 2 * k) % cols) for i in range(cols)])  2.32 us
    ppermute x6, starting transfers between devices, partner(): return lax.ppermute(x, 'col', [(i, i ^ 1) for i in range(cols)])  0.87 us
  transfers between devices with their start and end apart: 16, of which 4 were waited for; matrix products, arithmetic and copies ran while one was open for 1% of the time, Pallas kernels for 23%

profile of v3, /device:TPU:0, one launch (start us, length us, event | category | flops | bytes accessed | tf_op | source)
XLA Modules:
  0.0 35.0 jit_solution(6717316402325863216)
XLA Ops:
  0.6 0.8 %shard_map.75 = (bf16[2,128,128]{2,1,0:T(8,128)(2,1)S(1)}, f32[64,128]{1,0:T(8,128)S(1)}, f32[64,128]{1,0:T(8,128)S(1)}) custom-call(f32[64,128]{1,0:T(8,128)} %left.1, f32[64,128]{1,0:T(8,128)} %right.1, bf16[64,128]{1,0:T(8,128)(2,1)} %left_panel.1, bf16[64,128]{1,0:T(8,128)(2,1)} %right_panel.1), custom_call_target="tpu_custom_call" | custom-call | bytes 28672 | tf_op jit(solution)/shard_map/pallas_call | solution.py:321
  1.5 3.1 %collective-permute-start = (bf16[2,128,128]{2,1,0:T(8,128)(2,1)S(1)}, bf16[2,128,128]{2,1,0:T(8,128)(2,1)S(1)}, u32[]{:S(2)}, u32[]{:S(2)}) collective-permute-start(bf16[2,128,128]{2,1,0:T(8,128)(2,1)S(1)} %get-tuple-element.48), channel_id=1, source_target_pairs={{0,2},{1,3},{2,4},{3,5},{4,6},{5,7},{6,0},{7,1},{8,10},{9,11},{10,... | collective-permute-start | bytes 196616 | tf_op jit(solution)/shard_map/ppermute | solution.py:340
  4.6 2.6 %collective-permute-start.1 = (bf16[2,128,128]{2,1,0:T(8,128)(2,1)S(1)}, bf16[2,128,128]{2,1,0:T(8,128)(2,1)S(1)}, u32[]{:S(2)}, u32[]{:S(2)}) collective-permute-start(bf16[2,128,128]{2,1,0:T(8,128)(2,1)S(1)} %get-tuple-element.48), channel_id=1, source_target_pairs={{0,4},{1,5},{2,6},{3,7},{4,0},{5,1},{6,2},{7,3},{8,12},{9,13},{10,... | collective-permute-start | bytes 196616 | tf_op jit(solution)/shard_map/ppermute | solution.py:340
  7.2 1.3 %collective-permute-start.2 = (bf16[2,128,128]{2,1,0:T(8,128)(2,1)S(1)}, bf16[2,128,128]{2,1,0:T(8,128)(2,1)S(1)}, u32[]{:S(2)}, u32[]{:S(2)}) collective-permute-start(bf16[2,128,128]{2,1,0:T(8,128)(2,1)S(1)} %get-tuple-element.48), channel_id=1, source_target_pairs={{0,6},{1,7},{2,0},{3,1},{4,2},{5,3},{6,4},{7,5},{8,14},{9,15},{10,... | collective-permute-start | bytes 196616 | tf_op jit(solution)/shard_map/ppermute | solution.py:340
  8.5 1.5 %collective-permute-start.4 = (bf16[2,128,128]{2,1,0:T(8,128)(2,1)S(1)}, bf16[2,128,128]{2,1,0:T(8,128)(2,1)S(1)}, u32[]{:S(2)}, u32[]{:S(2)}) collective-permute-start(bf16[2,128,128]{2,1,0:T(8,128)(2,1)S(1)} %get-tuple-element.48), channel_id=1, source_target_pairs={{0,8},{8,0},{16,24},{24,16},{1,9},{9,1},{17,25},{25,17},{2,10},{10... | collective-permute-start | bytes 196616 | tf_op jit(solution)/shard_map/ppermute | solution.py:346
  10.0 1.5 %collective-permute-start.7 = (bf16[2,128,128]{2,1,0:T(8,128)(2,1)S(1)}, bf16[2,128,128]{2,1,0:T(8,128)(2,1)S(1)}, u32[]{:S(2)}, u32[]{:S(2)}) collective-permute-start(bf16[2,128,128]{2,1,0:T(8,128)(2,1)S(1)} %get-tuple-element.48), channel_id=1, source_target_pairs={{0,16},{8,24},{16,0},{24,8},{1,17},{9,25},{17,1},{25,9},{2,18},{10... | collective-permute-start | bytes 196616 | tf_op jit(solution)/shard_map/ppermute | solution.py:346
  11.5 0.5 %collective-permute-start.10 = (bf16[2,128,128]{2,1,0:T(8,128)(2,1)S(1)}, bf16[2,128,128]{2,1,0:T(8,128)(2,1)S(1)}, u32[]{:S(2)}, u32[]{:S(2)}) collective-permute-start(bf16[2,128,128]{2,1,0:T(8,128)(2,1)S(1)} %get-tuple-element.48), channel_id=1, source_target_pairs={{0,24},{8,16},{16,8},{24,0},{1,25},{9,17},{17,9},{25,1},{2,26},{10... | collective-permute-start | bytes 196616 | tf_op jit(solution)/shard_map/ppermute | solution.py:346
  12.2 1.6 %collective-permute-start.5 = (bf16[2,384,128]{2,1,0:T(8,128)(2,1)S(1)}, bf16[2,384,128]{2,1,0:T(8,128)(2,1)S(1)}, u32[]{:S(2)}, u32[]{:S(2)}) collective-permute-start(bf16[2,384,128]{2,1,0:T(8,128)(2,1)S(1)} %get-tuple-element.90), channel_id=1, source_target_pairs={{0,8},{8,0},{16,24},{24,16},{1,9},{9,1},{17,25},{25,17},{2,10},{10... | collective-permute-start | bytes 589832 | tf_op jit(solution)/shard_map/ppermute | solution.py:346
  13.7 1.5 %collective-permute-start.8 = (bf16[2,384,128]{2,1,0:T(8,128)(2,1)S(1)}, bf16[2,384,128]{2,1,0:T(8,128)(2,1)S(1)}, u32[]{:S(2)}, u32[]{:S(2)}) collective-permute-start(bf16[2,384,128]{2,1,0:T(8,128)(2,1)S(1)} %get-tuple-element.90), channel_id=1, source_target_pairs={{0,16},{8,24},{16,0},{24,8},{1,17},{9,25},{17,1},{25,9},{2,18},{10... | collective-permute-start | bytes 589832 | tf_op jit(solution)/shard_map/ppermute | solution.py:346
  15.4 2.1 %collective-permute-done.10 = bf16[2,128,128]{2,1,0:T(8,128)(2,1)S(1)} collective-permute-done((bf16[2,128,128]{2,1,0:T(8,128)(2,1)S(1)}, bf16[2,128,128]{2,1,0:T(8,128)(2,1)S(1)}, u32[]{:S(2)}, u32[]{:S(2)}) %collective-permute-start.10) | collective-permute-done | bytes 65568 | tf_op jit(solution)/shard_map/ppermute | solution.py:346
  18.1 1.6 %collective-permute-done.5 = bf16[2,384,128]{2,1,0:T(8,128)(2,1)S(1)} collective-permute-done((bf16[2,384,128]{2,1,0:T(8,128)(2,1)S(1)}, bf16[2,384,128]{2,1,0:T(8,128)(2,1)S(1)}, u32[]{:S(2)}, u32[]{:S(2)}) %collective-permute-start.5) | collective-permute-done | bytes 196640 | tf_op jit(solution)/shard_map/ppermute | solution.py:346
  19.8 1.8 %collective-permute-done.8 = bf16[2,384,128]{2,1,0:T(8,128)(2,1)S(1)} collective-permute-done((bf16[2,384,128]{2,1,0:T(8,128)(2,1)S(1)}, bf16[2,384,128]{2,1,0:T(8,128)(2,1)S(1)}, u32[]{:S(2)}, u32[]{:S(2)}) %collective-permute-start.8) | collective-permute-done | bytes 196640 | tf_op jit(solution)/shard_map/ppermute | solution.py:346
  21.7 2.3 %collective-permute-done.11 = bf16[2,128,128]{2,1,0:T(8,128)(2,1)S(1)} collective-permute-done((bf16[2,128,128]{2,1,0:T(8,128)(2,1)S(1)}, bf16[2,128,128]{2,1,0:T(8,128)(2,1)S(1)}, u32[]{:S(2)}, u32[]{:S(2)}) %collective-permute-start.11) | collective-permute-done | bytes 65568 | tf_op jit(solution)/shard_map/ppermute | solution.py:340
  24.2 0.5 %shard_map.76 = (f32[8,256,256]{2,1,0:T(8,128)S(1)}, f32[4,256,256]{2,1,0:T(8,128)S(1)}, f32[8,256,128]{2,1,0:T(8,128)S(1)}, f32[4,8,256]{2,1,0:T(8,128)S(1)}) custom-call(bf16[2,4,128,128]{3,2,1,0:T(8,128)(2,1)S(1)} %bitcast.8), custom_call_target="tpu_custom_call" | custom-call | flops 100663296 | bytes 561152 | tf_op jit(solution)/shard_map/pallas_call | solution.py:321
  24.7 0.5 %shard_map.77 = (f32[8,256,256]{2,1,0:T(8,128)S(1)}, f32[4,256,256]{2,1,0:T(8,128)S(1)}, f32[8,256,128]{2,1,0:T(8,128)S(1)}, f32[4,8,256]{2,1,0:T(8,128)S(1)}) custom-call(bf16[2,4,128,128]{3,2,1,0:T(8,128)(2,1)S(1)} %bitcast.9, bf16[2,4,128,128]{3,2,1,0:T(8,128)(2,1)S(1)} %bitcast.26, ...), custom_call_target="tpu_custom_call", output_to_operand_aliasing={{0}: (2, {}), {1}: (3, {}), {2}: (4, {}), {3}: (5, {})} | custom-call | flops 100663296 | bytes 1122304 | tf_op jit(solution)/shard_map/pallas_call | solution.py:321
  25.2 0.9 %shard_map.78 = (f32[8,256,256]{2,1,0:T(8,128)S(1)}, f32[4,256,256]{2,1,0:T(8,128)S(1)}, f32[8,256,128]{2,1,0:T(8,128)S(1)}, f32[4,8,256]{2,1,0:T(8,128)S(1)}) custom-call(bf16[2,4,128,128]{3,2,1,0:T(8,128)(2,1)S(1)} %bitcast.10, bf16[2,4,128,128]{3,2,1,0:T(8,128)(2,1)S(1)} %bitcast.27, ...), custom_call_target="tpu_custom_call", output_to_operand_aliasing={{0}: (3, {}), {1}: (4, {}), {2}: (5, {}), {3}: (6, {})} | custom-call | flops 402653184 | bytes 1155072 | tf_op jit(solution)/shard_map/pallas_call | solution.py:321
  26.1 1.1 %shard_map.79 = (f32[8,256,256]{2,1,0:T(8,128)S(1)}, f32[4,256,256]{2,1,0:T(8,128)S(1)}, f32[8,256,128]{2,1,0:T(8,128)S(1)}, f32[4,8,256]{2,1,0:T(8,128)S(1)}) custom-call(bf16[2,4,128,128]{3,2,1,0:T(8,128)(2,1)S(1)} %bitcast.11, bf16[2,4,128,128]{3,2,1,0:T(8,128)(2,1)S(1)} %bitcast.28, ...), custom_call_target="tpu_custom_call", output_to_operand_aliasing={{0}: (4, {}), {1}: (5, {}), {2}: (6, {}), {3}: (7, {})} | custom-call | flops 603979776 | bytes 1187840 | tf_op jit(solution)/shard_map/pallas_call | solution.py:321
  27.2 1.0 %shard_map.80 = (f32[8,256,256]{2,1,0:T(8,128)S(1)}, f32[4,256,256]{2,1,0:T(8,128)S(1)}, f32[8,256,128]{2,1,0:T(8,128)S(1)}, f32[4,8,256]{2,1,0:T(8,128)S(1)}) custom-call(bf16[2,4,128,128]{3,2,1,0:T(8,128)(2,1)S(1)} %bitcast.12, bf16[2,4,128,128]{3,2,1,0:T(8,128)(2,1)S(1)} %bitcast.21, ...), custom_call_target="tpu_custom_call", output_to_operand_aliasing={{0}: (5, {}), {1}: (6, {}), {2}: (7, {}), {3}: (8, {})} | custom-call | flops 603979776 | bytes 1220608 | tf_op jit(solution)/shard_map/pallas_call | solution.py:321
  28.3 1.3 %shard_map.81 = (f32[8,256,256]{2,1,0:T(8,128)S(1)}, f32[4,256,256]{2,1,0:T(8,128)S(1)}, f32[8,256,128]{2,1,0:T(8,128)S(1)}, f32[4,8,256]{2,1,0:T(8,128)S(1)}, b...) custom-call(bf16[2,4,128,128]{3,2,1,0:T(8,128)(2,1)S(1)} %bitcast.13, ...), custom_call_target="tpu_custom_call", output_to_operand_aliasing={{0}: (7, {}), {1}: (8, {}), {2}: (9, {}), {3}: (10, {})} | custom-call | flops 1006632960 | bytes 1449984 | tf_op jit(solution)/shard_map/pallas_call | solution.py:321
  29.6 0.8 %shard_map.82 = (bf16[2048,128]{1,0:T(8,128)(2,1)S(1)}, f32[2048,128]{1,0:T(8,128)S(1)}, f32[64,128]{1,0:T(8,128)S(1)}, bf16[256,1024]{1,0:T(8,128)(2,1)S(1)}) custom-call(f32[64,128]{1,0:T(8,128)S(1)} %get-tuple-element.72.points_left, f32[8,256,256]{2,1,0:T(8,128)S(1)} %get-tuple-element.73.left_sum, f32[4,8,256]{2,1,0:T(8,128)S(1)} %get-tuple-element.74.right_norm, ...), custom_call_target="tpu_custom_call" | custom-call | bytes 798720 | tf_op jit(solution)/shard_map/pallas_call | solution.py:321
  30.4 0.6 %collective-permute-start.15 = (bf16[2048,128]{1,0:T(8,128)(2,1)S(1)}, bf16[2048,128]{1,0:T(8,128)(2,1)S(1)}, u32[]{:S(2)}, u32[]{:S(2)}) collective-permute-start(bf16[2048,128]{1,0:T(8,128)(2,1)S(1)} %get-tuple-element.78), channel_id=1, source_target_pairs={{0,1},{1,0},{2,3},{3,2},{4,5},{5,4},{6,7},{7,6},{8,9},{9,8},{10,11... | collective-permute-start | bytes 1572872 | tf_op jit(solution)/shard_map/ppermute | solution.py:349
  31.0 1.2 %shard_map.83 = (bf16[1024,128]{1,0:T(8,128)(2,1)S(1)}, f32[8,1024]{1,0:T(8,128)S(1)}, f32[64,128]{1,0:T(8,128)S(1)}) custom-call(f32[64,128]{1,0:T(8,128)S(1)} %get-tuple-element.47.points_right, f32[4,256,256]{2,1,0:T(8,128)S(1)} %get-tuple-element.69.right_sum, bf16[1536,256]{1,0:T(8,128)(2,1)S(1)} %get-tuple-element.70.refs_0_, ...), custom_call_target="tpu_custom_call" | custom-call | bytes 667648 | tf_op jit(solution)/shard_map/pallas_call | solution.py:321
  32.8 1.0 %shard_map.86 = (f32[64,128]{1,0:T(8,128)S(1)}, f32[64,128]{1,0:T(8,128)S(1)}, f32[64,128]{1,0:T(8,128)S(1)}, f32[64,128]{1,0:T(8,128)S(1)}) custom-call(f32[2048,128]{1,0:T(8,128)S(1)} %get-tuple-element.77.base, bf16[2048,128]{1,0:T(8,128)(2,1)S(1)} %collective-permute-done.15.came, bf16[1024,128]{1,0:T(8,128)(2,1)S(1)} %get-tuple-element.76.sent, ...), custom_call_target="tpu_custom_call" | custom-call | bytes 389120 | tf_op jit(solution)/shard_map/pallas_call | solution.py:321
  33.8 1.2 %shard_map.87 = (f32[64,128]{1,0:T(8,128)}, f32[64,128]{1,0:T(8,128)}, f32[64,128]{1,0:T(8,128)}, f32[64,128]{1,0:T(8,128)}) custom-call(bf16[1024,128]{1,0:T(8,128)(2,1)S(1)} %collective-permute-done.14.came, f32[64,128]{1,0:T(8,128)S(1)} %get-tuple-element.86.left_value, f32[64,128]{1,0:T(8,128)S(1)} %get-tuple-element.87.left_term, ...), custom_call_target="tpu_custom_call" | custom-call | bytes 131072 | tf_op jit(solution)/shard_map/pallas_call | solution.py:321
  (33 shorter events, 1.7 us)
Async XLA Ops:
  1.5 10.1 %collective-permute-start = (bf16[2,128,128]{2,1,0:T(8,128)(2,1)S(1)}, bf16[2,128,128]{2,1,0:T(8,128)(2,1)S(1)}, u32[]{:S(2)}, u32[]{:S(2)}) collective-permute-start(bf16[2,128,128]{2,1,0:T(8,128)(2,1)S(1)} %get-tuple-element.48), channel_id=1, source_target_pairs={{0,2},{1,3},{2,4},{3,5},{4,6},{5,7},{6,0},{7,1},{8,10},{9,11},{10,... | collective-permute-start | bytes 196616 | tf_op jit(solution)/shard_map/ppermute | solution.py:340
  4.6 7.5 %collective-permute-start.1 = (bf16[2,128,128]{2,1,0:T(8,128)(2,1)S(1)}, bf16[2,128,128]{2,1,0:T(8,128)(2,1)S(1)}, u32[]{:S(2)}, u32[]{:S(2)}) collective-permute-start(bf16[2,128,128]{2,1,0:T(8,128)(2,1)S(1)} %get-tuple-element.48), channel_id=1, source_target_pairs={{0,4},{1,5},{2,6},{3,7},{4,0},{5,1},{6,2},{7,3},{8,12},{9,13},{10,... | collective-permute-start | bytes 196616 | tf_op jit(solution)/shard_map/ppermute | solution.py:340
  7.2 5.0 %collective-permute-start.2 = (bf16[2,128,128]{2,1,0:T(8,128)(2,1)S(1)}, bf16[2,128,128]{2,1,0:T(8,128)(2,1)S(1)}, u32[]{:S(2)}, u32[]{:S(2)}) collective-permute-start(bf16[2,128,128]{2,1,0:T(8,128)(2,1)S(1)} %get-tuple-element.48), channel_id=1, source_target_pairs={{0,6},{1,7},{2,0},{3,1},{4,2},{5,3},{6,4},{7,5},{8,14},{9,15},{10,... | collective-permute-start | bytes 196616 | tf_op jit(solution)/shard_map/ppermute | solution.py:340
  8.5 6.8 %collective-permute-start.4 = (bf16[2,128,128]{2,1,0:T(8,128)(2,1)S(1)}, bf16[2,128,128]{2,1,0:T(8,128)(2,1)S(1)}, u32[]{:S(2)}, u32[]{:S(2)}) collective-permute-start(bf16[2,128,128]{2,1,0:T(8,128)(2,1)S(1)} %get-tuple-element.48), channel_id=1, source_target_pairs={{0,8},{8,0},{16,24},{24,16},{1,9},{9,1},{17,25},{25,17},{2,10},{10... | collective-permute-start | bytes 196616 | tf_op jit(solution)/shard_map/ppermute | solution.py:346
  10.0 8.0 %collective-permute-start.7 = (bf16[2,128,128]{2,1,0:T(8,128)(2,1)S(1)}, bf16[2,128,128]{2,1,0:T(8,128)(2,1)S(1)}, u32[]{:S(2)}, u32[]{:S(2)}) collective-permute-start(bf16[2,128,128]{2,1,0:T(8,128)(2,1)S(1)} %get-tuple-element.48), channel_id=1, source_target_pairs={{0,16},{8,24},{16,0},{24,8},{1,17},{9,25},{17,1},{25,9},{2,18},{10... | collective-permute-start | bytes 196616 | tf_op jit(solution)/shard_map/ppermute | solution.py:346
  11.5 6.0 %collective-permute-start.10 = (bf16[2,128,128]{2,1,0:T(8,128)(2,1)S(1)}, bf16[2,128,128]{2,1,0:T(8,128)(2,1)S(1)}, u32[]{:S(2)}, u32[]{:S(2)}) collective-permute-start(bf16[2,128,128]{2,1,0:T(8,128)(2,1)S(1)} %get-tuple-element.48), channel_id=1, source_target_pairs={{0,24},{8,16},{16,8},{24,0},{1,25},{9,17},{17,9},{25,1},{2,26},{10... | collective-permute-start | bytes 196616 | tf_op jit(solution)/shard_map/ppermute | solution.py:346
  12.2 7.5 %collective-permute-start.5 = (bf16[2,384,128]{2,1,0:T(8,128)(2,1)S(1)}, bf16[2,384,128]{2,1,0:T(8,128)(2,1)S(1)}, u32[]{:S(2)}, u32[]{:S(2)}) collective-permute-start(bf16[2,384,128]{2,1,0:T(8,128)(2,1)S(1)} %get-tuple-element.90), channel_id=1, source_target_pairs={{0,8},{8,0},{16,24},{24,16},{1,9},{9,1},{17,25},{25,17},{2,10},{10... | collective-permute-start | bytes 589832 | tf_op jit(solution)/shard_map/ppermute | solution.py:346
  13.7 7.9 %collective-permute-start.8 = (bf16[2,384,128]{2,1,0:T(8,128)(2,1)S(1)}, bf16[2,384,128]{2,1,0:T(8,128)(2,1)S(1)}, u32[]{:S(2)}, u32[]{:S(2)}) collective-permute-start(bf16[2,384,128]{2,1,0:T(8,128)(2,1)S(1)} %get-tuple-element.90), channel_id=1, source_target_pairs={{0,16},{8,24},{16,0},{24,8},{1,17},{9,25},{17,1},{25,9},{2,18},{10... | collective-permute-start | bytes 589832 | tf_op jit(solution)/shard_map/ppermute | solution.py:346
  15.3 9.4 %collective-permute-start.3 = (bf16[2,512,128]{2,1,0:T(8,128)(2,1)S(1)}, bf16[2,512,128]{2,1,0:T(8,128)(2,1)S(1)}, u32[]{:S(2)}, u32[]{:S(2)}) collective-permute-start(bf16[2,512,128]{2,1,0:T(8,128)(2,1)S(1)} %get-tuple-element.91), channel_id=1, source_target_pairs={{0,1},{1,0},{2,3},{3,2},{4,5},{5,4},{6,7},{7,6},{8,9},{9,8},{10,11... | collective-permute-start | bytes 786440 | tf_op jit(solution)/shard_map/ppermute | solution.py:349
  17.5 6.6 %collective-permute-start.12 = (bf16[2,256,128]{2,1,0:T(8,128)(2,1)S(1)}, bf16[2,256,128]{2,1,0:T(8,128)(2,1)S(1)}, u32[]{:S(2)}, u32[]{:S(2)}) collective-permute-start(bf16[2,256,128]{2,1,0:T(8,128)(2,1)S(1)} %pad_maximum_fusion), channel_id=1, source_target_pairs={{0,24},{8,16},{16,8},{24,0},{1,25},{9,17},{17,9},{25,1},{2,26},{10... | collective-permute-start | bytes 393224 | tf_op jit(solution)/shard_map/ppermute | solution.py:346
  17.9 6.1 %collective-permute-start.11 = (bf16[2,128,128]{2,1,0:T(8,128)(2,1)S(1)}, bf16[2,128,128]{2,1,0:T(8,128)(2,1)S(1)}, u32[]{:S(2)}, u32[]{:S(2)}) collective-permute-start(bf16[2,128,128]{2,1,0:T(8,128)(2,1)S(1)} %collective-permute-done.10), channel_id=1, source_target_pairs={{0,2},{1,3},{2,4},{3,5},{4,6},{5,7},{6,0},{7,1},{8,10},{9,11},{10,... | collective-permute-start | bytes 196616 | tf_op jit(solution)/shard_map/ppermute | solution.py:340
  19.8 7.5 %collective-permute-start.6 = (bf16[2,512,128]{2,1,0:T(8,128)(2,1)S(1)}, bf16[2,512,128]{2,1,0:T(8,128)(2,1)S(1)}, u32[]{:S(2)}, u32[]{:S(2)}) collective-permute-start(bf16[2,512,128]{2,1,0:T(8,128)(2,1)S(1)} %constant_dynamic-update-slice_fusion.7), channel_id=1, source_target_pairs={{0,1},{1,0},{2,3},{3,2},{4,5},{5,4},{6,7},{7,6},{8,9},{9,8},{10,11... | collective-permute-start | bytes 786440 | tf_op jit(solution)/shard_map/ppermute | solution.py:349
  21.7 5.6 %collective-permute-start.9 = (bf16[2,512,128]{2,1,0:T(8,128)(2,1)S(1)}, bf16[2,512,128]{2,1,0:T(8,128)(2,1)S(1)}, u32[]{:S(2)}, u32[]{:S(2)}) collective-permute-start(bf16[2,512,128]{2,1,0:T(8,128)(2,1)S(1)} %constant_dynamic-update-slice_fusion.9), channel_id=1, source_target_pairs={{0,1},{1,0},{2,3},{3,2},{4,5},{5,4},{6,7},{7,6},{8,9},{9,8},{10,11... | collective-permute-start | bytes 786440 | tf_op jit(solution)/shard_map/ppermute | solution.py:349
  24.1 5.5 %collective-permute-start.13 = (bf16[2,512,128]{2,1,0:T(8,128)(2,1)S(1)}, bf16[2,512,128]{2,1,0:T(8,128)(2,1)S(1)}, u32[]{:S(2)}, u32[]{:S(2)}) collective-permute-start(bf16[2,512,128]{2,1,0:T(8,128)(2,1)S(1)} %constant_dynamic-update-slice_fusion.11), channel_id=1, source_target_pairs={{0,1},{1,0},{2,3},{3,2},{4,5},{5,4},{6,7},{7,6},{8,9},{9,8},{10,11... | collective-permute-start | bytes 786440 | tf_op jit(solution)/shard_map/ppermute | solution.py:349
  30.4 2.4 %collective-permute-start.15 = (bf16[2048,128]{1,0:T(8,128)(2,1)S(1)}, bf16[2048,128]{1,0:T(8,128)(2,1)S(1)}, u32[]{:S(2)}, u32[]{:S(2)}) collective-permute-start(bf16[2048,128]{1,0:T(8,128)(2,1)S(1)} %get-tuple-element.78), channel_id=1, source_target_pairs={{0,1},{1,0},{2,3},{3,2},{4,5},{5,4},{6,7},{7,6},{8,9},{9,8},{10,11... | collective-permute-start | bytes 1572872 | tf_op jit(solution)/shard_map/ppermute | solution.py:349
  32.2 1.6 %collective-permute-start.14 = (bf16[1024,128]{1,0:T(8,128)(2,1)S(1)}, bf16[1024,128]{1,0:T(8,128)(2,1)S(1)}, u32[]{:S(2)}, u32[]{:S(2)}) collective-permute-start(bf16[1024,128]{1,0:T(8,128)(2,1)S(1)} %get-tuple-element.76.sent), channel_id=1, source_target_pairs={{0,1},{1,0},{2,3},{3,2},{4,5},{5,4},{6,7},{7,6},{8,9},{9,8},{10,11... | collective-permute-start | bytes 786440 | tf_op jit(solution)/shard_map/ppermute | solution.py:349

commit v4 on v3

--- a/solution.py
+++ b/solution.py
@@ -165,7 +165,7 @@
     for k in new_right:
         right_norm[k] = exp2_scale * norm_row(rows_of(blocks[k, 0], 1, 0))
     for index, (lefts, rights) in enumerate(rects):
-        product = outs[4 + index] if keep else outs[4]
+        product = outs[4 + keep.index(index)] if index in keep else outs[-1]
         products(blocks, lefts, rights, place, left_norm, right_norm, product)
         others = ones_rows(blocks, [(k, 0) for k in rights], 1)
         size = others.shape[0] // len(rights)
@@ -178,7 +178,7 @@
                 left_sum[place(left)] = term
             else:
                 left_sum[place(left)] += term
-        if keep:
+        if index in keep:
             continue
         others = ones_rows(blocks, lefts, 0)
         for n, k in enumerate(rights):
@@ -379,22 +379,22 @@
     values = None
     seen_left, seen_right = set(), set()
 
-    def stage(rects, new_left, new_right, keep=False):
+    def stage(rects, new_left, new_right, keep=()):
         nonlocal values
         sets = sorted({x for lefts, _ in rects for x in lefts} | {(k, 0) for _, rights in rects for k in rights})
         lefts = {x for part, _ in rects for x in part}
         rights = {k for _, part in rects for k in part}
         plan = (rects, new_left, new_right, lefts - seen_left, rights - seen_right, values is None, keep)
         seen_left.update(lefts)
-        if not keep:
-            seen_right.update(rights)
+        seen_right.update(k for i, (_, part) in enumerate(rects) if i not in keep for k in part)
         places = [(len(a) * size, len(b) * size) for a, b in rects]
+        inner = [x for i, x in enumerate(places) if i not in keep]
         inputs = [blocks[x] for x in sets] + list(values or ())
         values = call(
             functools.partial(stage_kernel, plan, sets),
             inputs,
-            state + tuple(shape(x, bf16) for x in places if keep),
-            [] if keep else [pltpu.VMEM(tuple(max(x) for x in zip(*places)), bf16)],
+            state + tuple(shape(places[i], bf16) for i in keep),
+            [pltpu.VMEM(tuple(max(x) for x in zip(*inner)), bf16)] if inner else [],
             aliases={len(sets) + i: i for i in range(4)} if values else None,
             flops=sum(len(a) * len(b) for a, b in rects) * 12 * size * size * width,
         )
@@ -415,16 +415,16 @@
             held = weights([(i, half) for half in (0, 1) for i in range(k)])
         old = [(i, half) for half in (0, 1) for i in range(k) if (i, half) in seen_left]
         rects = ([(old, [k])] if old else []) + [([(k, 0)], list(range(k + 1)))]
-        stage(rects, [(k, 0)], [k], keep=k == rows - 1)
+        stage(rects, [(k, 0)], [k], keep=(0,) if k == rows - 1 else ())
         if k == rows - 1:
-            kept, values, pieces = values[4:], values[:4], rects
+            kept, values, pieces = values[4:], values[:4], rects[:1]
         waiting.append((k, 1))
         if k != 1 and k != rows - 1:
             stage([(waiting, list(range(k + 1)))], waiting, [])
             waiting = []
     if waiting[:-1]:
         more = [(waiting[:-1], list(range(rows)))]
-        stage(more, waiting[:-1], [], keep=True)
+        stage(more, waiting[:-1], [], keep=(0,))
         kept, values, pieces = [*kept, *values[4:]], values[:4], pieces + more
     left_sum, right_sum, _, right_norm = values
     near = [blocks[k, 0] for k in range(rows)]

time: 35.2 us -> 35.1 us (level)
  no operation moved by 1% of the time
where the time goes in v4:
time: 35.1 us; the launch traced here: 34.9 us
  starting transfers between devices  15.1 us (43%)
  Pallas kernels  10.8 us (31%)
  waiting for transfers between devices  7.89 us (22%)
  between operations  0.87 us (2%)
    pallas_call x13, Pallas kernels, call(): pl.pallas_call(kernel, out_shape=tuple(outputs), in_specs=[pl.BlockSpec(m...  10.8 us
    ppermute x4, starting transfers between devices, along_col(): lax.ppermute(x, 'col', [(i, (i + 2 * k) % cols) for i in range(cols)])  7.19 us
    ppermute x6, starting transfers between devices, along_row(): return lax.ppermute(x, 'row', [(i, target(i)) for i in range(rows)])  7.07 us
    ppermute x6, waiting for transfers between devices, along_row(): return lax.ppermute(x, 'row', [(i, target(i)) for i in range(rows)])  5.55 us
    ppermute x4, waiting for transfers between devices, along_col(): lax.ppermute(x, 'col', [(i, (i + 2 * k) % cols) for i in range(cols)])  2.32 us
    ppermute x6, starting transfers between devices, partner(): return lax.ppermute(x, 'col', [(i, i ^ 1) for i in range(cols)])  0.87 us
  transfers between devices with their start and end apart: 16, of which 4 were waited for; matrix products, arithmetic and copies ran while one was open for 1% of the time, Pallas kernels for 23%

profile of v4, /device:TPU:0, one launch (start us, length us, event | category | flops | bytes accessed | tf_op | source)
XLA Modules:
  0.0 34.9 jit_solution(14076605376476106854)
XLA Ops:
  0.6 0.8 %shard_map.75 = (bf16[2,128,128]{2,1,0:T(8,128)(2,1)S(1)}, f32[64,128]{1,0:T(8,128)S(1)}, f32[64,128]{1,0:T(8,128)S(1)}) custom-call(f32[64,128]{1,0:T(8,128)} %left.1, f32[64,128]{1,0:T(8,128)} %right.1, bf16[64,128]{1,0:T(8,128)(2,1)} %left_panel.1, bf16[64,128]{1,0:T(8,128)(2,1)} %right_panel.1), custom_call_target="tpu_custom_call" | custom-call | bytes 28672 | tf_op jit(solution)/shard_map/pallas_call | solution.py:321
  1.5 3.1 %collective-permute-start = (bf16[2,128,128]{2,1,0:T(8,128)(2,1)S(1)}, bf16[2,128,128]{2,1,0:T(8,128)(2,1)S(1)}, u32[]{:S(2)}, u32[]{:S(2)}) collective-permute-start(bf16[2,128,128]{2,1,0:T(8,128)(2,1)S(1)} %get-tuple-element.47), channel_id=1, source_target_pairs={{0,2},{1,3},{2,4},{3,5},{4,6},{5,7},{6,0},{7,1},{8,10},{9,11},{10,... | collective-permute-start | bytes 196616 | tf_op jit(solution)/shard_map/ppermute | solution.py:340
  4.6 2.6 %collective-permute-start.1 = (bf16[2,128,128]{2,1,0:T(8,128)(2,1)S(1)}, bf16[2,128,128]{2,1,0:T(8,128)(2,1)S(1)}, u32[]{:S(2)}, u32[]{:S(2)}) collective-permute-start(bf16[2,128,128]{2,1,0:T(8,128)(2,1)S(1)} %get-tuple-element.47), channel_id=1, source_target_pairs={{0,4},{1,5},{2,6},{3,7},{4,0},{5,1},{6,2},{7,3},{8,12},{9,13},{10,... | collective-permute-start | bytes 196616 | tf_op jit(solution)/shard_map/ppermute | solution.py:340
  7.2 1.3 %collective-permute-start.2 = (bf16[2,128,128]{2,1,0:T(8,128)(2,1)S(1)}, bf16[2,128,128]{2,1,0:T(8,128)(2,1)S(1)}, u32[]{:S(2)}, u32[]{:S(2)}) collective-permute-start(bf16[2,128,128]{2,1,0:T(8,128)(2,1)S(1)} %get-tuple-element.47), channel_id=1, source_target_pairs={{0,6},{1,7},{2,0},{3,1},{4,2},{5,3},{6,4},{7,5},{8,14},{9,15},{10,... | collective-permute-start | bytes 196616 | tf_op jit(solution)/shard_map/ppermute | solution.py:340
  8.5 1.5 %collective-permute-start.4 = (bf16[2,128,128]{2,1,0:T(8,128)(2,1)S(1)}, bf16[2,128,128]{2,1,0:T(8,128)(2,1)S(1)}, u32[]{:S(2)}, u32[]{:S(2)}) collective-permute-start(bf16[2,128,128]{2,1,0:T(8,128)(2,1)S(1)} %get-tuple-element.47), channel_id=1, source_target_pairs={{0,8},{8,0},{16,24},{24,16},{1,9},{9,1},{17,25},{25,17},{2,10},{10... | collective-permute-start | bytes 196616 | tf_op jit(solution)/shard_map/ppermute | solution.py:346
  10.0 1.5 %collective-permute-start.7 = (bf16[2,128,128]{2,1,0:T(8,128)(2,1)S(1)}, bf16[2,128,128]{2,1,0:T(8,128)(2,1)S(1)}, u32[]{:S(2)}, u32[]{:S(2)}) collective-permute-start(bf16[2,128,128]{2,1,0:T(8,128)(2,1)S(1)} %get-tuple-element.47), channel_id=1, source_target_pairs={{0,16},{8,24},{16,0},{24,8},{1,17},{9,25},{17,1},{25,9},{2,18},{10... | collective-permute-start | bytes 196616 | tf_op jit(solution)/shard_map/ppermute | solution.py:346
  11.5 0.5 %collective-permute-start.10 = (bf16[2,128,128]{2,1,0:T(8,128)(2,1)S(1)}, bf16[2,128,128]{2,1,0:T(8,128)(2,1)S(1)}, u32[]{:S(2)}, u32[]{:S(2)}) collective-permute-start(bf16[2,128,128]{2,1,0:T(8,128)(2,1)S(1)} %get-tuple-element.47), channel_id=1, source_target_pairs={{0,24},{8,16},{16,8},{24,0},{1,25},{9,17},{17,9},{25,1},{2,26},{10... | collective-permute-start | bytes 196616 | tf_op jit(solution)/shard_map/ppermute | solution.py:346
  12.2 1.6 %collective-permute-start.5 = (bf16[2,384,128]{2,1,0:T(8,128)(2,1)S(1)}, bf16[2,384,128]{2,1,0:T(8,128)(2,1)S(1)}, u32[]{:S(2)}, u32[]{:S(2)}) collective-permute-start(bf16[2,384,128]{2,1,0:T(8,128)(2,1)S(1)} %get-tuple-element.88), channel_id=1, source_target_pairs={{0,8},{8,0},{16,24},{24,16},{1,9},{9,1},{17,25},{25,17},{2,10},{10... | collective-permute-start | bytes 589832 | tf_op jit(solution)/shard_map/ppermute | solution.py:346
  13.7 1.5 %collective-permute-start.8 = (bf16[2,384,128]{2,1,0:T(8,128)(2,1)S(1)}, bf16[2,384,128]{2,1,0:T(8,128)(2,1)S(1)}, u32[]{:S(2)}, u32[]{:S(2)}) collective-permute-start(bf16[2,384,128]{2,1,0:T(8,128)(2,1)S(1)} %get-tuple-element.88), channel_id=1, source_target_pairs={{0,16},{8,24},{16,0},{24,8},{1,17},{9,25},{17,1},{25,9},{2,18},{10... | collective-permute-start | bytes 589832 | tf_op jit(solution)/shard_map/ppermute | solution.py:346
  15.4 2.1 %collective-permute-done.10 = bf16[2,128,128]{2,1,0:T(8,128)(2,1)S(1)} collective-permute-done((bf16[2,128,128]{2,1,0:T(8,128)(2,1)S(1)}, bf16[2,128,128]{2,1,0:T(8,128)(2,1)S(1)}, u32[]{:S(2)}, u32[]{:S(2)}) %collective-permute-start.10) | collective-permute-done | bytes 65568 | tf_op jit(solution)/shard_map/ppermute | solution.py:346
  18.1 1.6 %collective-permute-done.5 = bf16[2,384,128]{2,1,0:T(8,128)(2,1)S(1)} collective-permute-done((bf16[2,384,128]{2,1,0:T(8,128)(2,1)S(1)}, bf16[2,384,128]{2,1,0:T(8,128)(2,1)S(1)}, u32[]{:S(2)}, u32[]{:S(2)}) %collective-permute-start.5) | collective-permute-done | bytes 196640 | tf_op jit(solution)/shard_map/ppermute | solution.py:346
  19.8 1.8 %collective-permute-done.8 = bf16[2,384,128]{2,1,0:T(8,128)(2,1)S(1)} collective-permute-done((bf16[2,384,128]{2,1,0:T(8,128)(2,1)S(1)}, bf16[2,384,128]{2,1,0:T(8,128)(2,1)S(1)}, u32[]{:S(2)}, u32[]{:S(2)}) %collective-permute-start.8) | collective-permute-done | bytes 196640 | tf_op jit(solution)/shard_map/ppermute | solution.py:346
  21.7 2.3 %collective-permute-done.11 = bf16[2,128,128]{2,1,0:T(8,128)(2,1)S(1)} collective-permute-done((bf16[2,128,128]{2,1,0:T(8,128)(2,1)S(1)}, bf16[2,128,128]{2,1,0:T(8,128)(2,1)S(1)}, u32[]{:S(2)}, u32[]{:S(2)}) %collective-permute-start.11) | collective-permute-done | bytes 65568 | tf_op jit(solution)/shard_map/ppermute | solution.py:340
  24.2 0.5 %shard_map.76 = (f32[8,256,256]{2,1,0:T(8,128)S(1)}, f32[4,256,256]{2,1,0:T(8,128)S(1)}, f32[8,256,128]{2,1,0:T(8,128)S(1)}, f32[4,8,256]{2,1,0:T(8,128)S(1)}) custom-call(bf16[2,4,128,128]{3,2,1,0:T(8,128)(2,1)S(1)} %bitcast.8), custom_call_target="tpu_custom_call" | custom-call | flops 100663296 | bytes 561152 | tf_op jit(solution)/shard_map/pallas_call | solution.py:321
  24.7 0.5 %shard_map.77 = (f32[8,256,256]{2,1,0:T(8,128)S(1)}, f32[4,256,256]{2,1,0:T(8,128)S(1)}, f32[8,256,128]{2,1,0:T(8,128)S(1)}, f32[4,8,256]{2,1,0:T(8,128)S(1)}) custom-call(bf16[2,4,128,128]{3,2,1,0:T(8,128)(2,1)S(1)} %bitcast.9, bf16[2,4,128,128]{3,2,1,0:T(8,128)(2,1)S(1)} %bitcast.26, ...), custom_call_target="tpu_custom_call", output_to_operand_aliasing={{0}: (2, {}), {1}: (3, {}), {2}: (4, {}), {3}: (5, {})} | custom-call | flops 100663296 | bytes 1122304 | tf_op jit(solution)/shard_map/pallas_call | solution.py:321
  25.2 0.9 %shard_map.78 = (f32[8,256,256]{2,1,0:T(8,128)S(1)}, f32[4,256,256]{2,1,0:T(8,128)S(1)}, f32[8,256,128]{2,1,0:T(8,128)S(1)}, f32[4,8,256]{2,1,0:T(8,128)S(1)}) custom-call(bf16[2,4,128,128]{3,2,1,0:T(8,128)(2,1)S(1)} %bitcast.10, bf16[2,4,128,128]{3,2,1,0:T(8,128)(2,1)S(1)} %bitcast.27, ...), custom_call_target="tpu_custom_call", output_to_operand_aliasing={{0}: (3, {}), {1}: (4, {}), {2}: (5, {}), {3}: (6, {})} | custom-call | flops 402653184 | bytes 1155072 | tf_op jit(solution)/shard_map/pallas_call | solution.py:321
  26.1 1.1 %shard_map.79 = (f32[8,256,256]{2,1,0:T(8,128)S(1)}, f32[4,256,256]{2,1,0:T(8,128)S(1)}, f32[8,256,128]{2,1,0:T(8,128)S(1)}, f32[4,8,256]{2,1,0:T(8,128)S(1)}) custom-call(bf16[2,4,128,128]{3,2,1,0:T(8,128)(2,1)S(1)} %bitcast.11, bf16[2,4,128,128]{3,2,1,0:T(8,128)(2,1)S(1)} %bitcast.28, ...), custom_call_target="tpu_custom_call", output_to_operand_aliasing={{0}: (4, {}), {1}: (5, {}), {2}: (6, {}), {3}: (7, {})} | custom-call | flops 603979776 | bytes 1187840 | tf_op jit(solution)/shard_map/pallas_call | solution.py:321
  27.2 1.0 %shard_map.80 = (f32[8,256,256]{2,1,0:T(8,128)S(1)}, f32[4,256,256]{2,1,0:T(8,128)S(1)}, f32[8,256,128]{2,1,0:T(8,128)S(1)}, f32[4,8,256]{2,1,0:T(8,128)S(1)}) custom-call(bf16[2,4,128,128]{3,2,1,0:T(8,128)(2,1)S(1)} %bitcast.12, bf16[2,4,128,128]{3,2,1,0:T(8,128)(2,1)S(1)} %bitcast.21, ...), custom_call_target="tpu_custom_call", output_to_operand_aliasing={{0}: (5, {}), {1}: (6, {}), {2}: (7, {}), {3}: (8, {})} | custom-call | flops 603979776 | bytes 1220608 | tf_op jit(solution)/shard_map/pallas_call | solution.py:321
  28.3 1.4 %shard_map.81 = (f32[8,256,256]{2,1,0:T(8,128)S(1)}, f32[4,256,256]{2,1,0:T(8,128)S(1)}, f32[8,256,128]{2,1,0:T(8,128)S(1)}, f32[4,8,256]{2,1,0:T(8,128)S(1)}, bf16[1536,256]{1,0:T(8,128)(2,1)S(1)}) custom-call(bf16[2,4,128,128]{3,2,1,0:T(8,128)(2,1)S(1)} %bitcast.13, ...), custom_call_target="tpu_custom_call", output_to_operand_aliasing={{0}: (7, {}), {1}: (8, {}), {2}: (9, {}), {3}: (10, {})} | custom-call | flops 1006632960 | bytes 1384448 | tf_op jit(solution)/shard_map/pallas_call | solution.py:321
  29.7 0.8 %shard_map.82 = (bf16[2048,128]{1,0:T(8,128)(2,1)S(1)}, f32[2048,128]{1,0:T(8,128)S(1)}, f32[64,128]{1,0:T(8,128)S(1)}, bf16[256,1024]{1,0:T(8,128)(2,1)S(1)}) custom-call(f32[64,128]{1,0:T(8,128)S(1)} %get-tuple-element.70.points_left, f32[8,256,256]{2,1,0:T(8,128)S(1)} %get-tuple-element.71.left_sum, f32[4,8,256]{2,1,0:T(8,128)S(1)} %get-tuple-element.72.right_norm, ...), custom_call_target="tpu_custom_call" | custom-call | bytes 798720 | tf_op jit(solution)/shard_map/pallas_call | solution.py:321
  30.5 0.6 %collective-permute-start.15 = (bf16[2048,128]{1,0:T(8,128)(2,1)S(1)}, bf16[2048,128]{1,0:T(8,128)(2,1)S(1)}, u32[]{:S(2)}, u32[]{:S(2)}) collective-permute-start(bf16[2048,128]{1,0:T(8,128)(2,1)S(1)} %get-tuple-element.76), channel_id=1, source_target_pairs={{0,1},{1,0},{2,3},{3,2},{4,5},{5,4},{6,7},{7,6},{8,9},{9,8},{10,11... | collective-permute-start | bytes 1572872 | tf_op jit(solution)/shard_map/ppermute | solution.py:349
  31.0 1.1 %shard_map.83 = (bf16[1024,128]{1,0:T(8,128)(2,1)S(1)}, f32[8,1024]{1,0:T(8,128)S(1)}, f32[64,128]{1,0:T(8,128)S(1)}) custom-call(f32[64,128]{1,0:T(8,128)S(1)} %get-tuple-element.46.points_right, f32[4,256,256]{2,1,0:T(8,128)S(1)} %get-tuple-element.68.right_sum, bf16[1536,256]{1,0:T(8,128)(2,1)S(1)} %get-tuple-element.69.refs_0_, ...), custom_call_target="tpu_custom_call" | custom-call | bytes 602112 | tf_op jit(solution)/shard_map/pallas_call | solution.py:321
  32.7 1.0 %shard_map.86 = (f32[64,128]{1,0:T(8,128)S(1)}, f32[64,128]{1,0:T(8,128)S(1)}, f32[64,128]{1,0:T(8,128)S(1)}, f32[64,128]{1,0:T(8,128)S(1)}) custom-call(f32[2048,128]{1,0:T(8,128)S(1)} %get-tuple-element.75.base, bf16[2048,128]{1,0:T(8,128)(2,1)S(1)} %collective-permute-done.15.came, bf16[1024,128]{1,0:T(8,128)(2,1)S(1)} %get-tuple-element.74.sent, ...), custom_call_target="tpu_custom_call" | custom-call | bytes 389120 | tf_op jit(solution)/shard_map/pallas_call | solution.py:321
  33.7 1.2 %shard_map.87 = (f32[64,128]{1,0:T(8,128)}, f32[64,128]{1,0:T(8,128)}, f32[64,128]{1,0:T(8,128)}, f32[64,128]{1,0:T(8,128)}) custom-call(bf16[1024,128]{1,0:T(8,128)(2,1)S(1)} %collective-permute-done.14.came, f32[64,128]{1,0:T(8,128)S(1)} %get-tuple-element.84.left_value, f32[64,128]{1,0:T(8,128)S(1)} %get-tuple-element.85.left_term, ...), custom_call_target="tpu_custom_call" | custom-call | bytes 131072 | tf_op jit(solution)/shard_map/pallas_call | solution.py:321
  (33 shorter events, 1.7 us)
Async XLA Ops:
  1.5 10.1 %collective-permute-start = (bf16[2,128,128]{2,1,0:T(8,128)(2,1)S(1)}, bf16[2,128,128]{2,1,0:T(8,128)(2,1)S(1)}, u32[]{:S(2)}, u32[]{:S(2)}) collective-permute-start(bf16[2,128,128]{2,1,0:T(8,128)(2,1)S(1)} %get-tuple-element.47), channel_id=1, source_target_pairs={{0,2},{1,3},{2,4},{3,5},{4,6},{5,7},{6,0},{7,1},{8,10},{9,11},{10,... | collective-permute-start | bytes 196616 | tf_op jit(solution)/shard_map/ppermute | solution.py:340
  4.6 7.5 %collective-permute-start.1 = (bf16[2,128,128]{2,1,0:T(8,128)(2,1)S(1)}, bf16[2,128,128]{2,1,0:T(8,128)(2,1)S(1)}, u32[]{:S(2)}, u32[]{:S(2)}) collective-permute-start(bf16[2,128,128]{2,1,0:T(8,128)(2,1)S(1)} %get-tuple-element.47), channel_id=1, source_target_pairs={{0,4},{1,5},{2,6},{3,7},{4,0},{5,1},{6,2},{7,3},{8,12},{9,13},{10,... | collective-permute-start | bytes 196616 | tf_op jit(solution)/shard_map/ppermute | solution.py:340
  7.2 5.0 %collective-permute-start.2 = (bf16[2,128,128]{2,1,0:T(8,128)(2,1)S(1)}, bf16[2,128,128]{2,1,0:T(8,128)(2,1)S(1)}, u32[]{:S(2)}, u32[]{:S(2)}) collective-permute-start(bf16[2,128,128]{2,1,0:T(8,128)(2,1)S(1)} %get-tuple-element.47), channel_id=1, source_target_pairs={{0,6},{1,7},{2,0},{3,1},{4,2},{5,3},{6,4},{7,5},{8,14},{9,15},{10,... | collective-permute-start | bytes 196616 | tf_op jit(solution)/shard_map/ppermute | solution.py:340
  8.5 6.8 %collective-permute-start.4 = (bf16[2,128,128]{2,1,0:T(8,128)(2,1)S(1)}, bf16[2,128,128]{2,1,0:T(8,128)(2,1)S(1)}, u32[]{:S(2)}, u32[]{:S(2)}) collective-permute-start(bf16[2,128,128]{2,1,0:T(8,128)(2,1)S(1)} %get-tuple-element.47), channel_id=1, source_target_pairs={{0,8},{8,0},{16,24},{24,16},{1,9},{9,1},{17,25},{25,17},{2,10},{10... | collective-permute-start | bytes 196616 | tf_op jit(solution)/shard_map/ppermute | solution.py:346
  10.0 8.0 %collective-permute-start.7 = (bf16[2,128,128]{2,1,0:T(8,128)(2,1)S(1)}, bf16[2,128,128]{2,1,0:T(8,128)(2,1)S(1)}, u32[]{:S(2)}, u32[]{:S(2)}) collective-permute-start(bf16[2,128,128]{2,1,0:T(8,128)(2,1)S(1)} %get-tuple-element.47), channel_id=1, source_target_pairs={{0,16},{8,24},{16,0},{24,8},{1,17},{9,25},{17,1},{25,9},{2,18},{10... | collective-permute-start | bytes 196616 | tf_op jit(solution)/shard_map/ppermute | solution.py:346
  11.5 6.0 %collective-permute-start.10 = (bf16[2,128,128]{2,1,0:T(8,128)(2,1)S(1)}, bf16[2,128,128]{2,1,0:T(8,128)(2,1)S(1)}, u32[]{:S(2)}, u32[]{:S(2)}) collective-permute-start(bf16[2,128,128]{2,1,0:T(8,128)(2,1)S(1)} %get-tuple-element.47), channel_id=1, source_target_pairs={{0,24},{8,16},{16,8},{24,0},{1,25},{9,17},{17,9},{25,1},{2,26},{10... | collective-permute-start | bytes 196616 | tf_op jit(solution)/shard_map/ppermute | solution.py:346
  12.2 7.5 %collective-permute-start.5 = (bf16[2,384,128]{2,1,0:T(8,128)(2,1)S(1)}, bf16[2,384,128]{2,1,0:T(8,128)(2,1)S(1)}, u32[]{:S(2)}, u32[]{:S(2)}) collective-permute-start(bf16[2,384,128]{2,1,0:T(8,128)(2,1)S(1)} %get-tuple-element.88), channel_id=1, source_target_pairs={{0,8},{8,0},{16,24},{24,16},{1,9},{9,1},{17,25},{25,17},{2,10},{10... | collective-permute-start | bytes 589832 | tf_op jit(solution)/shard_map/ppermute | solution.py:346
  13.7 7.9 %collective-permute-start.8 = (bf16[2,384,128]{2,1,0:T(8,128)(2,1)S(1)}, bf16[2,384,128]{2,1,0:T(8,128)(2,1)S(1)}, u32[]{:S(2)}, u32[]{:S(2)}) collective-permute-start(bf16[2,384,128]{2,1,0:T(8,128)(2,1)S(1)} %get-tuple-element.88), channel_id=1, source_target_pairs={{0,16},{8,24},{16,0},{24,8},{1,17},{9,25},{17,1},{25,9},{2,18},{10... | collective-permute-start | bytes 589832 | tf_op jit(solution)/shard_map/ppermute | solution.py:346
  15.3 9.4 %collective-permute-start.3 = (bf16[2,512,128]{2,1,0:T(8,128)(2,1)S(1)}, bf16[2,512,128]{2,1,0:T(8,128)(2,1)S(1)}, u32[]{:S(2)}, u32[]{:S(2)}) collective-permute-start(bf16[2,512,128]{2,1,0:T(8,128)(2,1)S(1)} %get-tuple-element.89), channel_id=1, source_target_pairs={{0,1},{1,0},{2,3},{3,2},{4,5},{5,4},{6,7},{7,6},{8,9},{9,8},{10,11... | collective-permute-start | bytes 786440 | tf_op jit(solution)/shard_map/ppermute | solution.py:349
  17.5 6.6 %collective-permute-start.12 = (bf16[2,256,128]{2,1,0:T(8,128)(2,1)S(1)}, bf16[2,256,128]{2,1,0:T(8,128)(2,1)S(1)}, u32[]{:S(2)}, u32[]{:S(2)}) collective-permute-start(bf16[2,256,128]{2,1,0:T(8,128)(2,1)S(1)} %pad_maximum_fusion), channel_id=1, source_target_pairs={{0,24},{8,16},{16,8},{24,0},{1,25},{9,17},{17,9},{25,1},{2,26},{10... | collective-permute-start | bytes 393224 | tf_op jit(solution)/shard_map/ppermute | solution.py:346
  17.9 6.1 %collective-permute-start.11 = (bf16[2,128,128]{2,1,0:T(8,128)(2,1)S(1)}, bf16[2,128,128]{2,1,0:T(8,128)(2,1)S(1)}, u32[]{:S(2)}, u32[]{:S(2)}) collective-permute-start(bf16[2,128,128]{2,1,0:T(8,128)(2,1)S(1)} %collective-permute-done.10), channel_id=1, source_target_pairs={{0,2},{1,3},{2,4},{3,5},{4,6},{5,7},{6,0},{7,1},{8,10},{9,11},{10,... | collective-permute-start | bytes 196616 | tf_op jit(solution)/shard_map/ppermute | solution.py:340
  19.8 7.5 %collective-permute-start.6 = (bf16[2,512,128]{2,1,0:T(8,128)(2,1)S(1)}, bf16[2,512,128]{2,1,0:T(8,128)(2,1)S(1)}, u32[]{:S(2)}, u32[]{:S(2)}) collective-permute-start(bf16[2,512,128]{2,1,0:T(8,128)(2,1)S(1)} %constant_dynamic-update-slice_fusion.7), channel_id=1, source_target_pairs={{0,1},{1,0},{2,3},{3,2},{4,5},{5,4},{6,7},{7,6},{8,9},{9,8},{10,11... | collective-permute-start | bytes 786440 | tf_op jit(solution)/shard_map/ppermute | solution.py:349
  21.7 5.6 %collective-permute-start.9 = (bf16[2,512,128]{2,1,0:T(8,128)(2,1)S(1)}, bf16[2,512,128]{2,1,0:T(8,128)(2,1)S(1)}, u32[]{:S(2)}, u32[]{:S(2)}) collective-permute-start(bf16[2,512,128]{2,1,0:T(8,128)(2,1)S(1)} %constant_dynamic-update-slice_fusion.9), channel_id=1, source_target_pairs={{0,1},{1,0},{2,3},{3,2},{4,5},{5,4},{6,7},{7,6},{8,9},{9,8},{10,11... | collective-permute-start | bytes 786440 | tf_op jit(solution)/shard_map/ppermute | solution.py:349
  24.1 5.5 %collective-permute-start.13 = (bf16[2,512,128]{2,1,0:T(8,128)(2,1)S(1)}, bf16[2,512,128]{2,1,0:T(8,128)(2,1)S(1)}, u32[]{:S(2)}, u32[]{:S(2)}) collective-permute-start(bf16[2,512,128]{2,1,0:T(8,128)(2,1)S(1)} %constant_dynamic-update-slice_fusion.11), channel_id=1, source_target_pairs={{0,1},{1,0},{2,3},{3,2},{4,5},{5,4},{6,7},{7,6},{8,9},{9,8},{10,11... | collective-permute-start | bytes 786440 | tf_op jit(solution)/shard_map/ppermute | solution.py:349
  30.5 2.2 %collective-permute-start.15 = (bf16[2048,128]{1,0:T(8,128)(2,1)S(1)}, bf16[2048,128]{1,0:T(8,128)(2,1)S(1)}, u32[]{:S(2)}, u32[]{:S(2)}) collective-permute-start(bf16[2048,128]{1,0:T(8,128)(2,1)S(1)} %get-tuple-element.76), channel_id=1, source_target_pairs={{0,1},{1,0},{2,3},{3,2},{4,5},{5,4},{6,7},{7,6},{8,9},{9,8},{10,11... | collective-permute-start | bytes 1572872 | tf_op jit(solution)/shard_map/ppermute | solution.py:349
  32.1 1.6 %collective-permute-start.14 = (bf16[1024,128]{1,0:T(8,128)(2,1)S(1)}, bf16[1024,128]{1,0:T(8,128)(2,1)S(1)}, u32[]{:S(2)}, u32[]{:S(2)}) collective-permute-start(bf16[1024,128]{1,0:T(8,128)(2,1)S(1)} %get-tuple-element.74.sent), channel_id=1, source_target_pairs={{0,1},{1,0},{2,3},{3,2},{4,5},{5,4},{6,7},{7,6},{8,9},{9,8},{10,11... | collective-permute-start | bytes 786440 | tf_op jit(solution)/shard_map/ppermute | solution.py:349
